TPU v7x, 256 devices: a whole 4x4x8 slice. The times are simulated.
256 devices in a mesh: dp: 4 (over x), seq: 64 (over z, y, core).
Axes of the slice: x: 4, y: 4, z: 8, core: 2. Of those that a mesh axis runs over, the one named last changes fastest.
Arguments:
- query_gate: bfloat16 [4, 8192, 4096], P('dp', 'seq'), may hold values from -6 to 6
- key_gate: bfloat16 [4, 8192, 4096], P('dp', 'seq'), may hold values from -6 to 6
- value_feat: bfloat16 [4, 8192, 4096], P('dp', 'seq'), may hold values from -6 to 6
- filters: bfloat16 [256, 128], replicated, may hold values from -0.5 to 0.5
- grad_out: bfloat16 [4, 8192, 4096], P('dp', 'seq'), may hold values from -6 to 6
- basis_prev: float32 [128, 16], replicated, may hold values from -6 to 6
Outputs:
- mixed_out: bfloat16 [4, 8192, 4096], P('dp', 'seq')
- grad_query: bfloat16 [4, 8192, 4096], P('dp', 'seq')
- grad_key: bfloat16 [4, 8192, 4096], P('dp', 'seq')
- grad_value: bfloat16 [4, 8192, 4096], P('dp', 'seq')
- low_rank_grad: float32 [256, 128], replicated
- basis_next: float32 [128, 16], replicated
All inputs are finite; a program needn't handle non-finite values.
Results may differ from a plain program's by a relative error of at most 0.0061.
Values may be sent and summed in bfloat16 or wider, within the bound.
No kernel may reach another device: no remote copies, remote signals or barrier semaphores. Data moves between devices by JAX's collectives and lax.ppermute only.
A program may use at most 192 MiB of HBM per device.

v0:
```python
import functools

import jax
import jax.numpy as jnp
import numpy as np
from jax import lax
from jax.experimental import pallas as pl
from jax.experimental.pallas import tpu as pltpu
from jax.sharding import Mesh
from jax.sharding import PartitionSpec as P

HIGH = lax.Precision.HIGHEST
LANES = 256
TILE = 16
GROUP = 16
GROUPS = LANES // GROUP
STEP = 1024
NN = (((1,), (0,)), ((), ()))
NT = (((1,), (1,)), ((), ()))
VMEM_LIMIT = 24 * 1024 * 1024


def dot(a, b, dims=NN, precision=None):
    return lax.dot_general(a, b, dims, precision=precision, preferred_element_type=jnp.float32)


def off_chip(x):
    return pltpu.with_memory_space_constraint(x, pltpu.HBM)


def gate_kernel(cotan_ref, query_ref, key_ref, value_ref, grad_ref, prod_ref):
    width = cotan_ref.shape[1]
    cols = pl.ds(pl.multiple_of(pl.program_id(0) * width, width), width)
    for a, b, out in ((cotan_ref, query_ref, grad_ref), (key_ref, value_ref, prod_ref)):
        out[:, cols] = (a[...].astype(jnp.float32) * b[...].astype(jnp.float32)).astype(jnp.bfloat16)


def gated(query, key, value, cotan, grad_half):
    tok, channels = query.shape
    half = channels // 2
    width = STEP
    steps = half // width
    grad_at = pl.BlockSpec((tok, width), lambda i: (0, grad_half * steps + i))
    prod_at = pl.BlockSpec((tok, width), lambda i: (0, (1 - grad_half) * steps + i))
    return pl.pallas_call(
        gate_kernel,
        grid=(steps,),
        in_specs=[grad_at, grad_at, prod_at, prod_at],
        out_specs=[pl.BlockSpec(memory_space=pltpu.VMEM)] * 2,
        out_shape=[jax.ShapeDtypeStruct((tok, half), jnp.bfloat16)] * 2,
        compiler_params=pltpu.CompilerParams(vmem_limit_bytes=VMEM_LIMIT),
        cost_estimate=pl.CostEstimate(
            flops=2 * tok * half, bytes_accessed=12 * tok * half, transcendentals=0
        ),
        name="gated",
    )(*map(off_chip, (cotan, query, key, value)))


def lag_block(rows, window, flip, mask):
    tok = rows.shape[0]
    turned = dot(flip, rows).astype(jnp.bfloat16)
    reach = tok + TILE
    total = jnp.zeros((GROUPS * TILE, reach), jnp.float32)
    for low in range(0, tok, TILE):
        spread = jnp.concatenate([turned[low : low + TILE]] * GROUPS, axis=0) * mask
        total += dot(spread, window[low : low + reach], NT)
    rest = jnp.zeros((GROUPS * TILE, LANES - reach), jnp.float32)
    wide = jnp.concatenate([total, rest], axis=1).reshape(GROUPS, TILE, LANES)
    return jnp.sum(pltpu.roll(wide, 0, 2, stride=1, stride_axis=1), axis=1)


def lag_kernel(
    keep_ref, prod_a, grad_a, after_ref, prod_b, grad_b, before_ref, mask_ref, flip_ref, turn_ref, out_ref
):
    taps = out_ref.shape[1]
    has_before = keep_ref[0].astype(jnp.bfloat16)
    has_after = keep_ref[1].astype(jnp.bfloat16)
    mask, flip = mask_ref[...], flip_ref[...]
    late = []
    for low in range(0, prod_a.shape[1], LANES):
        cols = slice(low, low + LANES)
        window = jnp.concatenate([grad_a[:, cols], after_ref[:, cols] * has_after], axis=0)
        lined = lag_block(prod_a[:, cols], window, flip, mask)
        first = low // GROUP
        out_ref[first : first + GROUPS, :] = pltpu.roll(lined, LANES - TILE + 1, 1)[:, :taps]
        window = jnp.concatenate([before_ref[:, cols] * has_before, prod_b[:, cols]], axis=0)
        late.append(lag_block(grad_b[:, cols], window, flip, mask))
    out_ref[len(late) * GROUPS :, :] = dot(jnp.concatenate(late, axis=0), turn_ref[...], precision=HIGH)


def lag_sums(keep, prod_a, grad_a, after, prod_b, grad_b, before, taps):
    tok, channels = prod_a.shape
    where = np.arange(LANES)
    mask = where[:, None] // TILE == where[None, :] // GROUP
    row = np.arange(tok)
    flip = row[:, None] // TILE * TILE + TILE - 1 - row[:, None] % TILE == row[None, :]
    turn = where[:, None] == tok + TILE - 1 - np.arange(taps)[None, :]
    fixed = [
        jnp.asarray(mask, jnp.bfloat16),
        jnp.asarray(flip, jnp.bfloat16),
        jnp.asarray(turn, jnp.float32),
    ]
    whole = pl.BlockSpec(memory_space=pltpu.VMEM)
    return pl.pallas_call(
        lag_kernel,
        in_specs=[pl.BlockSpec(memory_space=pltpu.SMEM)] + [whole] * (6 + len(fixed)),
        out_specs=whole,
        out_shape=jax.ShapeDtypeStruct((2 * channels // GROUP, taps), jnp.float32),
        compiler_params=pltpu.CompilerParams(vmem_limit_bytes=VMEM_LIMIT),
        cost_estimate=pl.CostEstimate(
            flops=2 * tok * 2 * channels * LANES * 16,
            bytes_accessed=12 * tok * channels,
            transcendentals=0,
        ),
        name="lag_sums",
    )(keep, prod_a, grad_a, after, prod_b, grad_b, before, *fixed)


def conv_block(window, line, shift, gates, outs, cols):
    tok = window.shape[0] // 2
    reach = tok + TILE
    line = line.astype(jnp.float32)
    line = jnp.concatenate([line, jnp.zeros_like(line)], axis=1)
    wide = jnp.broadcast_to(line[:, None, :], (GROUPS, TILE, LANES))
    table = pltpu.roll(wide, shift, 2, stride=1, stride_axis=1)
    table = table.reshape(GROUPS * TILE, LANES)[:, :reach].astype(jnp.bfloat16)
    lane_group = lax.broadcasted_iota(jnp.int32, (TILE, 128), 1) // GROUP
    for low in range(0, tok, TILE):
        full = dot(table, window[low : low + reach])
        rows = slice(low, low + TILE)
        for half in range(LANES // 128):
            conv = None
            for g in range(128 // GROUP):
                row = (half * (128 // GROUP) + g) * TILE
                mine = full[row : row + TILE, half * 128 : half * 128 + 128]
                conv = mine if conv is None else jnp.where(lane_group == g, mine, conv)
            lanes = slice(cols.start + half * 128, cols.start + half * 128 + 128)
            for gate, out in zip(gates, outs):
                out[rows, lanes] = (gate[rows, lanes].astype(jnp.float32) * conv).astype(jnp.bfloat16)


def conv_kernel(
    start, keep_ref, fwd_line, prod_ref, before_ref, query_ref, cotan_ref,
    bwd_line, grad_ref, after_ref, value_ref, key_ref, *refs
):
    mixed, grad_query, grad_key, grad_value = refs[-4:]
    has_before = keep_ref[0].astype(jnp.bfloat16)
    has_after = keep_ref[1].astype(jnp.bfloat16)
    width = query_ref.shape[1]
    step = pl.program_id(0) * width + start
    for low in range(0, width, LANES):
        cols = slice(low, low + LANES)
        here = pl.ds(pl.multiple_of(step + low, LANES), LANES)
        lines = slice(low // GROUP, low // GROUP + GROUPS)
        window = jnp.concatenate([before_ref[:, here] * has_before, prod_ref[:, here]], axis=0)
        conv_block(window, fwd_line[lines], 1, (query_ref, cotan_ref), (mixed, grad_query), cols)
        window = jnp.concatenate([grad_ref[:, here], after_ref[:, here] * has_after], axis=0)
        conv_block(window, bwd_line[lines], 0, (value_ref, key_ref), (grad_key, grad_value), cols)


def gated_convs(keep, taps, turned, prod, before, grad, after, gates, fwd_half, start, count, into):
    tok, channels = gates[0].shape
    half = channels // 2 // STEP
    fwd = fwd_half * half + start
    bwd = (1 - fwd_half) * half + start
    whole = pl.BlockSpec(memory_space=pltpu.VMEM)
    at_fwd = pl.BlockSpec((tok, STEP), lambda i: (0, fwd + i))
    at_bwd = pl.BlockSpec((tok, STEP), lambda i: (0, bwd + i))
    width = taps.shape[1]
    shape = jax.ShapeDtypeStruct((tok, channels), jnp.bfloat16)
    in_specs = [
        pl.BlockSpec(memory_space=pltpu.SMEM),
        pl.BlockSpec((STEP // GROUP, width), lambda i: (fwd + i, 0)), whole, whole, at_fwd, at_fwd,
        pl.BlockSpec((STEP // GROUP, width), lambda i: (bwd + i, 0)), whole, whole, at_bwd, at_bwd,
    ]
    query, key, value, cotan = map(off_chip, gates)
    args = [keep, turned, prod, before, query, cotan, taps, grad, after, value, key]
    aliases = {len(args) + n: n for n in range(len(into))}
    return pl.pallas_call(
        functools.partial(conv_kernel, start * STEP),
        grid=(count,),
        in_specs=in_specs + [pl.BlockSpec(memory_space=pl.ANY)] * len(into),
        out_specs=[at_fwd, at_fwd, at_bwd, at_bwd],
        out_shape=[shape] * 4,
        input_output_aliases=aliases,
        compiler_params=pltpu.CompilerParams(vmem_limit_bytes=VMEM_LIMIT),
        cost_estimate=pl.CostEstimate(
            flops=8 * count * tok * STEP * LANES * 16,
            bytes_accessed=24 * count * tok * STEP,
            transcendentals=0,
        ),
        name="gated_convs",
    )(*args, *into)


def low_rank_kernel(scale, grad_ref, basis_ref, low_ref, next_ref):
    grad = grad_ref[...]
    left = dot(basis_ref[...], grad, NT, HIGH)
    index = lax.broadcasted_iota(jnp.int32, left.shape, 0)
    rest = left
    ortho = jnp.zeros_like(left)
    for i in range(left.shape[0]):
        row = rest[i : i + 1]
        unit = row / jnp.sqrt(jnp.sum(row * row, axis=1, keepdims=True) + 1e-06)
        ortho = jnp.where(index == i, unit, ortho)
        coeff = jnp.sum(left * unit, axis=1, keepdims=True)
        rest = rest - coeff * unit
    right = dot(ortho, grad, NN, HIGH) * scale
    next_ref[...] = right
    low_ref[...] = dot(ortho, right, (((0,), (0,)), ((), ())), HIGH)


def low_rank(grad, basis, scale):
    return pl.pallas_call(
        functools.partial(low_rank_kernel, scale),
        out_shape=[
            jax.ShapeDtypeStruct(grad.shape, jnp.float32),
            jax.ShapeDtypeStruct(basis.shape, jnp.float32),
        ],
        compiler_params=pltpu.CompilerParams(vmem_limit_bytes=VMEM_LIMIT),
        name="low_rank",
    )(grad, basis)


def tie(*arrays):
    return lax.optimization_barrier(arrays)


def on_device(query_gate, key_gate, value_feat, filters, grad_out, basis_prev):
    query, key, value, cotan = query_gate[0], key_gate[0], value_feat[0], grad_out[0]
    tok, channels = query.shape
    groups, taps = filters.shape
    seq = ("z", "y", "core")
    near = ("dp", "y", "core")
    size = lax.axis_size(seq)
    place = lax.axis_index(seq)

    def from_next(x):
        return lax.ppermute(x, seq, [(i, (i - 1) % size) for i in range(size)])

    def from_last(x):
        return lax.ppermute(x, seq, [(i, (i + 1) % size) for i in range(size)])

    gates = (query, key, value, cotan)
    grad_a, prod_b = gated(*gates, 0)
    after_a, before_b = from_next(grad_a), from_last(prod_b)
    grad_b, prod_a = gated(*tie(*gates, grad_a, prod_b)[:4], 1)
    keep = jnp.stack([place > 0, place < size - 1]).astype(jnp.float32)
    turned = filters[:, ::-1]
    local = lag_sums(keep, prod_a, grad_a, after_a, prod_b, grad_b, before_b, taps)

    outs = ()

    def beside(start, given, windows, *which):
        nonlocal outs
        got = start(given)
        windows = tie(*windows, given)[:4]
        outs = gated_convs(keep, filters, turned, *windows, gates, *which, outs)
        got, *outs = tie(got, *outs)
        return got

    count = lax.axis_size(near)

    def exchanged(x):
        return lax.all_to_all(x, near, 0, 0, tiled=True)

    def hop(distance):
        route = [(i, i ^ distance) for i in range(lax.axis_size("z"))]
        return lambda x: lax.ppermute(x, "z", route)

    piece = beside(exchanged, local, (prod_b, before_b, grad_a, after_a), 1, 0, 2)
    piece = piece.reshape(count, groups // count, taps).sum(axis=0)
    grad_b, prod_a, _ = tie(grad_b, prod_a, piece)
    after_b, before_a = from_next(grad_b), from_last(prod_a)
    second = (prod_a, before_a, grad_b, after_b)
    piece = piece + hop(1)(piece)
    piece = piece + hop(2)(piece)
    piece = piece + beside(hop(4), piece, second, 0, 0, 1)
    spread = jnp.broadcast_to(piece[None], (count,) + piece.shape).reshape(groups, taps)
    filter_grad = beside(exchanged, spread, second, 0, 1, 1)
    scale = (lax.axis_size("dp") * size * tok * (channels // groups)) ** (-0.5)
    low, right = low_rank(filter_grad, basis_prev.T, scale)
    return (*[out[None] for out in outs], low, right.T)


def solution(mesh):
    dp = mesh.shape["dp"]
    fine = Mesh(mesh.devices.reshape(dp, -1, 4, 2), ("dp", "z", "y", "core"))
    split = P("dp", ("z", "y", "core"), None)
    return jax.shard_map(
        on_device,
        mesh=fine,
        in_specs=(split, split, split, P(), split, P()),
        out_specs=(split, split, split, split, P(), P()),
        check_vma=False,
    )
```

profile of v0, /device:TPU:1, one launch (start us, length us, event | category | flops | bytes accessed | tf_op | source)
XLA Modules:
  0.0 83.1 jit_solution(10934088133378814575)
XLA Ops:
  0.6 0.0 copy-start
  0.6 1.7 %gated.2 = (bf16[128,2048]{1,0:T(8,128)(2,1)S(1)}, bf16[128,2048]{1,0:T(8,128)(2,1)S(1)}) custom-call(bf16[128,4096]{1,0:T(8,128)(2,1)} %bitcast.19, bf16[128,4096]{1,0:T(8,128)(2,1)} %bitcast.24, bf16[128,4096]{1,0:T(8,128)(2,1)} %bitcast.29, bf16[128,4096]{1,0:T(8,128)(2,1)} %bitcast.34), custom_call_target="tpu_custom_call" | custom-call | flops 524288 | bytes 3145728 | tf_op jit(solution)/shard_map/gated/pallas_call | solution.py:45
  2.4 3.3 %collective-permute-start = (bf16[128,2048]{1,0:T(8,128)(2,1)S(1)}, bf16[128,2048]{1,0:T(8,128)(2,1)S(1)}, u32[]{:S(2)}, u32[]{:S(2)}) collective-permute-start(bf16[128,2048]{1,0:T(8,128)(2,1)S(1)} %get-tuple-element.67.grad_a.grad_ref), channel_id=1, source_target_pairs={{0,63},{1,0},{2,1},{3,2},{4,3},{5,4},{6,5},{7,6},{8,7},{9,8},{10,9... | collective-permute-start | bytes 1572872 | tf_op jit(solution)/shard_map/ppermute | solution.py:239
  5.7 0.0 collective-permute-start.1
  5.7 0.0 copy-done
  5.7 0.2 rev.3.fwd_line
  5.9 0.0 copy-start.2
  5.9 0.0 copy-start.3
  5.9 0.0 copy-start.4
  5.9 1.8 %gated.3 = (bf16[128,2048]{1,0:T(8,128)(2,1)S(1)}, bf16[128,2048]{1,0:T(8,128)(2,1)S(1)}) custom-call(bf16[128,4096]{1,0:T(8,128)(2,1)} %bitcast.20, bf16[128,4096]{1,0:T(8,128)(2,1)} %bitcast.25, bf16[128,4096]{1,0:T(8,128)(2,1)} %bitcast.30, bf16[128,4096]{1,0:T(8,128)(2,1)} %bitcast.35), custom_call_target="tpu_custom_call" | custom-call | flops 524288 | bytes 3145728 | tf_op jit(solution)/shard_map/gated/pallas_call | solution.py:45
  7.7 0.1 add_convert_fusion.keep_ref
  7.8 4.2 %collective-permute-done.after_ref = bf16[128,2048]{1,0:T(8,128)(2,1)S(1)} collective-permute-done((bf16[128,2048]{1,0:T(8,128)(2,1)S(1)}, bf16[128,2048]{1,0:T(8,128)(2,1)S(1)}, u32[]{:S(2)}, u32[]{:S(2)}) %collective-permute-start) | collective-permute-done | bytes 524320 | tf_op jit(solution)/shard_map/ppermute | solution.py:239
  12.0 1.1 %collective-permute-done.1.before_ref = bf16[128,2048]{1,0:T(8,128)(2,1)S(1)} collective-permute-done((bf16[128,2048]{1,0:T(8,128)(2,1)S(1)}, bf16[128,2048]{1,0:T(8,128)(2,1)S(1)}, u32[]{:S(2)}, u32[]{:S(2)}) %collective-permute-start.1) | collective-permute-done | bytes 524320 | tf_op jit(solution)/shard_map/ppermute | solution.py:242
  13.1 0.0 copy-done.2
  13.1 0.0 copy-done.3
  13.1 0.0 copy-done.4
  13.1 7.1 %lag_sums.1 = f32[256,128]{1,0:T(8,128)} custom-call(f32[2]{0:T(128)S(1)} %add_convert_fusion.keep_ref, bf16[128,2048]{1,0:T(8,128)(2,1)S(1)} %get-tuple-element.89.prod_a.prod_ref, bf16[128,2048]{1,0:T(8,128)(2,1)S(1)} %get-tuple-element.67.grad_a.grad_ref, bf16[128,2048]{1,0:T(8,128)(2,1)S(1)} %collective-permute-done.after_ref, ...), custom_call_target="tpu_custom_call" | custom-call | flops 4294967296 | bytes 3145728 | tf_op jit(solution)/shard_map/lag_sums/pallas_call | solution.py:104
  20.2 15.0 %all-to-all-start = ((f32[32,8,128]{2,1,0:T(8,128)}), f32[32,8,128]{2,1,0:T(8,128)S(1)}, u32[]{:S(2)}, u32[]{:S(2)}) async-start(f32[32,8,128]{2,1,0:T(8,128)} %bitcast.6), calls=%async_computation | async-start | bytes 262144 | tf_op jit(solution)/shard_map/all_to_all | solution.py:265
  35.2 6.9 %gated_convs.3 = (bf16[128,4096]{1,0:T(8,128)(2,1)}, bf16[128,4096]{1,0:T(8,128)(2,1)}, bf16[128,4096]{1,0:T(8,128)(2,1)}, bf16[128,4096]{1,0:T(8,128)(2,1)}) custom-call(f32[2]{0:T(128)S(1)} %add_convert_fusion.keep_ref, bf16[256,128]{1,0:T(8,128)(2,1)S(1)} %rev.3.fwd_line, bf16[128,2048]{1,0:T(8,128)(2,1)S(1)} %get-tuple-element.65.prod_b.prod_ref, ...), custom_call_target="tpu_custom_call" | custom-call | flops 8589934592 | bytes 6291456 | tf_op jit(solution)/shard_map/gated_convs/pallas_call | solution.py:179
  42.1 0.8 all-to-all-done
  43.0 0.9 %collective-permute-start.5 = (bf16[128,2048]{1,0:T(8,128)(2,1)S(1)}, bf16[128,2048]{1,0:T(8,128)(2,1)S(1)}, u32[]{:S(2)}, u32[]{:S(2)}) collective-permute-start(bf16[128,2048]{1,0:T(8,128)(2,1)S(1)} %get-tuple-element.89.prod_a.prod_ref), channel_id=1, source_target_pairs={{0,1},{1,2},{2,3},{3,4},{4,5},{5,6},{6,7},{7,8},{8,9},{9,10},{10,1... | collective-permute-start | bytes 1572872 | tf_op jit(solution)/shard_map/ppermute | solution.py:242
  43.9 0.0 collective-permute-start.6
  43.9 0.0 collective-permute-start.2
  43.9 2.5 %collective-permute-done.2 = f32[8,128]{1,0:T(8,128)S(1)} collective-permute-done((f32[8,128]{1,0:T(8,128)S(1)}, f32[8,128]{1,0:T(8,128)S(1)}, u32[]{:S(2)}, u32[]{:S(2)}) %collective-permute-start.2) | collective-permute-done | bytes 4128 | tf_op jit(solution)/shard_map/ppermute | solution.py:269
  46.3 0.0 collective-permute-start.3
  46.3 3.8 %collective-permute-done.3 = f32[8,128]{1,0:T(8,128)S(1)} collective-permute-done((f32[8,128]{1,0:T(8,128)S(1)}, f32[8,128]{1,0:T(8,128)S(1)}, u32[]{:S(2)}, u32[]{:S(2)}) %collective-permute-start.3) | collective-permute-done | bytes 4128 | tf_op jit(solution)/shard_map/ppermute | solution.py:269
  50.1 1.1 %collective-permute-start.4 = (f32[8,128]{1,0:T(8,128)S(1)}, f32[8,128]{1,0:T(8,128)S(1)}, u32[]{:S(2)}, u32[]{:S(2)}) collective-permute-start(f32[8,128]{1,0:T(8,128)S(1)} %add.18), channel_id=1, source_target_pairs={{0,32},{8,40},{16,48},{24,56},{32,0},{40,8},{48,16},{56,24},{1,33}... | collective-permute-start | bytes 12296 | tf_op jit(solution)/shard_map/ppermute | solution.py:269
  51.2 0.0 collective-permute-done.5.before_ref
  51.2 1.6 %collective-permute-done.6.after_ref = bf16[128,2048]{1,0:T(8,128)(2,1)S(1)} collective-permute-done((bf16[128,2048]{1,0:T(8,128)(2,1)S(1)}, bf16[128,2048]{1,0:T(8,128)(2,1)S(1)}, u32[]{:S(2)}, u32[]{:S(2)}) %collective-permute-start.6) | collective-permute-done | bytes 524320 | tf_op jit(solution)/shard_map/ppermute | solution.py:239
  52.8 4.4 %gated_convs.4 = (bf16[128,4096]{1,0:T(8,128)(2,1)}, bf16[128,4096]{1,0:T(8,128)(2,1)}, bf16[128,4096]{1,0:T(8,128)(2,1)}, bf16[128,4096]{1,0:T(8,128)(2,1)}) custom-call(f32[2]{0:T(128)S(1)} %add_convert_fusion.keep_ref, bf16[256,128]{1,0:T(8,128)(2,1)S(1)} %rev.3.fwd_line, ...), custom_call_target="tpu_custom_call", output_to_operand_aliasing={{0}: (11, {}), {1}: (12, {}), {2}: (13, {}), {3}: (14, {})} | custom-call | flops 4294967296 | bytes 3145728 | tf_op jit(solution)/shard_map/gated_convs/pallas_call | solution.py:179
  57.2 0.0 collective-permute-done.4
  57.2 0.7 broadcast_in_dim.18
  57.8 13.4 %all-to-all-start.1 = ((f32[32,8,128]{2,1,0:T(8,128)}), f32[32,8,128]{2,1,0:T(8,128)S(1)}, u32[]{:S(2)}, u32[]{:S(2)}) async-start(f32[32,8,128]{2,1,0:T(8,128)} %broadcast_in_dim.18), calls=%async_computation.1 | async-start | bytes 262144 | tf_op jit(solution)/shard_map/all_to_all | solution.py:265
  71.2 4.4 %gated_convs.5 = (bf16[128,4096]{1,0:T(8,128)(2,1)}, bf16[128,4096]{1,0:T(8,128)(2,1)}, bf16[128,4096]{1,0:T(8,128)(2,1)}, bf16[128,4096]{1,0:T(8,128)(2,1)}) custom-call(f32[2]{0:T(128)S(1)} %add_convert_fusion.keep_ref, bf16[256,128]{1,0:T(8,128)(2,1)S(1)} %rev.3.fwd_line, ...), custom_call_target="tpu_custom_call", output_to_operand_aliasing={{0}: (11, {}), {1}: (12, {}), {2}: (13, {}), {3}: (14, {})} | custom-call | flops 4294967296 | bytes 3145728 | tf_op jit(solution)/shard_map/gated_convs/pallas_call | solution.py:179
  75.6 0.0 copy-start.1
  75.6 3.3 %all-to-all-done.1 = f32[32,8,128]{2,1,0:T(8,128)S(1)} async-done(((f32[32,8,128]{2,1,0:T(8,128)}), f32[32,8,128]{2,1,0:T(8,128)S(1)}, u32[]{:S(2)}, u32[]{:S(2)}) %all-to-all-start.1) | async-done | bytes 131104 | tf_op jit(solution)/shard_map/all_to_all | solution.py:265
  78.9 0.0 copy-done.1
  78.9 4.1 %low_rank.1 = (f32[256,128]{1,0:T(8,128)}, f32[16,128]{1,0:T(8,128)}) custom-call(f32[256,128]{1,0:T(8,128)S(1)} %bitcast.17, f32[16,128]{1,0:T(8,128)S(1)} %bitcast.18), custom_call_target="tpu_custom_call" | custom-call | tf_op jit(solution)/shard_map/low_rank/pallas_call | solution.py:214
  (4 shorter events, 0.0 us)
Async XLA Ops:
  0.6 5.0 %copy-start = (bf16[256,128]{1,0:T(8,128)(2,1)S(1)}, bf16[256,128]{1,0:T(8,128)(2,1)}, u32[]{:S(2)}) copy-start(bf16[256,128]{1,0:T(8,128)(2,1)} %bwd_line.5) | copy-start | bytes 196612
  2.4 9.6 %collective-permute-start = (bf16[128,2048]{1,0:T(8,128)(2,1)S(1)}, bf16[128,2048]{1,0:T(8,128)(2,1)S(1)}, u32[]{:S(2)}, u32[]{:S(2)}) collective-permute-start(bf16[128,2048]{1,0:T(8,128)(2,1)S(1)} %get-tuple-element.67.grad_a.grad_ref), channel_id=1, source_target_pairs={{0,63},{1,0},{2,1},{3,2},{4,3},{5,4},{6,5},{7,6},{8,7},{9,8},{10,9... | collective-permute-start | bytes 1572872 | tf_op jit(solution)/shard_map/ppermute | solution.py:239
  5.7 7.4 %collective-permute-start.1 = (bf16[128,2048]{1,0:T(8,128)(2,1)S(1)}, bf16[128,2048]{1,0:T(8,128)(2,1)S(1)}, u32[]{:S(2)}, u32[]{:S(2)}) collective-permute-start(bf16[128,2048]{1,0:T(8,128)(2,1)S(1)} %get-tuple-element.65.prod_b.prod_ref), channel_id=1, source_target_pairs={{0,1},{1,2},{2,3},{3,4},{4,5},{5,6},{6,7},{7,8},{8,9},{9,10},{10,1... | collective-permute-start | bytes 1572872 | tf_op jit(solution)/shard_map/ppermute | solution.py:242
  5.9 7.2 %copy-start.2 = (bf16[256,256]{1,0:T(8,128)(2,1)S(1)}, bf16[256,256]{1,0:T(8,128)(2,1)}, u32[]{:S(2)}) copy-start(bf16[256,256]{1,0:T(8,128)(2,1)} %constant.28.clone.mask_ref) | copy-start | bytes 393220
  5.9 7.2 %copy-start.3 = (f32[256,128]{1,0:T(8,128)S(1)}, f32[256,128]{1,0:T(8,128)}, u32[]{:S(2)}) copy-start(f32[256,128]{1,0:T(8,128)} %constant.30.clone.turn_ref) | copy-start | bytes 393220
  5.9 7.2 %copy-start.4 = (bf16[128,128]{1,0:T(8,128)(2,1)S(1)}, bf16[128,128]{1,0:T(8,128)(2,1)}, u32[]{:S(2)}) copy-start(bf16[128,128]{1,0:T(8,128)(2,1)} %constant.29.clone.flip_ref) | copy-start | bytes 98308
  20.2 22.7 %all-to-all-start = ((f32[32,8,128]{2,1,0:T(8,128)}), f32[32,8,128]{2,1,0:T(8,128)S(1)}, u32[]{:S(2)}, u32[]{:S(2)}) async-start(f32[32,8,128]{2,1,0:T(8,128)} %bitcast.6), calls=%async_computation | async-start | bytes 262144 | tf_op jit(solution)/shard_map/all_to_all | solution.py:265
  43.0 8.2 %collective-permute-start.5 = (bf16[128,2048]{1,0:T(8,128)(2,1)S(1)}, bf16[128,2048]{1,0:T(8,128)(2,1)S(1)}, u32[]{:S(2)}, u32[]{:S(2)}) collective-permute-start(bf16[128,2048]{1,0:T(8,128)(2,1)S(1)} %get-tuple-element.89.prod_a.prod_ref), channel_id=1, source_target_pairs={{0,1},{1,2},{2,3},{3,4},{4,5},{5,6},{6,7},{7,8},{8,9},{9,10},{10,1... | collective-permute-start | bytes 1572872 | tf_op jit(solution)/shard_map/ppermute | solution.py:242
  43.9 8.9 %collective-permute-start.6 = (bf16[128,2048]{1,0:T(8,128)(2,1)S(1)}, bf16[128,2048]{1,0:T(8,128)(2,1)S(1)}, u32[]{:S(2)}, u32[]{:S(2)}) collective-permute-start(bf16[128,2048]{1,0:T(8,128)(2,1)S(1)} %get-tuple-element.91.grad_b.grad_ref), channel_id=1, source_target_pairs={{0,63},{1,0},{2,1},{3,2},{4,3},{5,4},{6,5},{7,6},{8,7},{9,8},{10,9... | collective-permute-start | bytes 1572872 | tf_op jit(solution)/shard_map/ppermute | solution.py:239
  43.9 2.5 %collective-permute-start.2 = (f32[8,128]{1,0:T(8,128)S(1)}, f32[8,128]{1,0:T(8,128)S(1)}, u32[]{:S(2)}, u32[]{:S(2)}) collective-permute-start(f32[8,128]{1,0:T(8,128)S(1)} %bitcast_reduce_fusion), channel_id=1, source_target_pairs={{0,8},{8,0},{16,24},{24,16},{32,40},{40,32},{48,56},{56,48},{1,9},... | collective-permute-start | bytes 12296 | tf_op jit(solution)/shard_map/ppermute | solution.py:269
  46.3 3.8 %collective-permute-start.3 = (f32[8,128]{1,0:T(8,128)S(1)}, f32[8,128]{1,0:T(8,128)S(1)}, u32[]{:S(2)}, u32[]{:S(2)}) collective-permute-start(f32[8,128]{1,0:T(8,128)S(1)} %add.17), channel_id=1, source_target_pairs={{0,16},{8,24},{16,0},{24,8},{32,48},{40,56},{48,32},{56,40},{1,17}... | collective-permute-start | bytes 12296 | tf_op jit(solution)/shard_map/ppermute | solution.py:269
  50.1 7.1 %collective-permute-start.4 = (f32[8,128]{1,0:T(8,128)S(1)}, f32[8,128]{1,0:T(8,128)S(1)}, u32[]{:S(2)}, u32[]{:S(2)}) collective-permute-start(f32[8,128]{1,0:T(8,128)S(1)} %add.18), channel_id=1, source_target_pairs={{0,32},{8,40},{16,48},{24,56},{32,0},{40,8},{48,16},{56,24},{1,33}... | collective-permute-start | bytes 12296 | tf_op jit(solution)/shard_map/ppermute | solution.py:269
  57.8 21.1 %all-to-all-start.1 = ((f32[32,8,128]{2,1,0:T(8,128)}), f32[32,8,128]{2,1,0:T(8,128)S(1)}, u32[]{:S(2)}, u32[]{:S(2)}) async-start(f32[32,8,128]{2,1,0:T(8,128)} %broadcast_in_dim.18), calls=%async_computation.1 | async-start | bytes 262144 | tf_op jit(solution)/shard_map/all_to_all | solution.py:265
  75.6 3.3 %copy-start.1 = (f32[128,16]{0,1:T(8,128)S(1)}, f32[128,16]{0,1:T(8,128)}, u32[]{:S(2)}) copy-start(f32[128,16]{0,1:T(8,128)} %param.14) | copy-start | bytes 24580
where the time goes:
time: 83.5 us; the launch traced here: 83.1 us
  starting transfers between devices  33.6 us (40%)
  Pallas kernels  30.5 us (37%)
  waiting for transfers between devices  17.2 us (21%)
  local copies, waits for them, and re-layouts  0.9 us (1%)
    all_to_all x2, starting transfers between devices, exchanged(): return lax.all_to_all(x, near, 0, 0, tiled=True)  28.3 us
    pallas_call x3, Pallas kernels, gated_convs(): pl.pallas_call(functools.partial(conv_kernel, start * STEP), grid=(count,...  15.7 us
    pallas_call x1, Pallas kernels, lag_sums(): pl.pallas_call(lag_kernel, in_specs=[pl.BlockSpec(memory_space=pltpu.SMEM...  7.14 us
    ppermute x3, waiting for transfers between devices, hop(): return lambda x: lax.ppermute(x, 'z', route)  6.22 us
    ppermute x2, waiting for transfers between devices, from_next(): return lax.ppermute(x, seq, [(i, (i - 1) % size) for i in range(size)])  5.82 us
    pallas_call x1, Pallas kernels, low_rank(): pl.pallas_call(functools.partial(low_rank_kernel, scale), out_shape=[jax....  4.15 us
    all_to_all x2, waiting for transfers between devices, exchanged(): return lax.all_to_all(x, near, 0, 0, tiled=True)  4.1 us
    pallas_call x2, Pallas kernels, gated(): pl.pallas_call(gate_kernel, grid=(steps,), in_specs=[grad_at, grad_at, pr...  3.46 us
  transfers between devices with their start and end apart: 9, of which 7 were waited for; matrix products, arithmetic and copies ran while one was open for 0% of the time, Pallas kernels for 21%

commit v1 on v0

--- a/solution.py
+++ b/solution.py
@@ -140,7 +140,7 @@
 
 
 def conv_kernel(
-    start, keep_ref, fwd_line, prod_ref, before_ref, query_ref, cotan_ref,
+    start, blocked, keep_ref, fwd_line, prod_ref, before_ref, query_ref, cotan_ref,
     bwd_line, grad_ref, after_ref, value_ref, key_ref, *refs
 ):
     mixed, grad_query, grad_key, grad_value = refs[-4:]
@@ -151,14 +151,15 @@
     for low in range(0, width, LANES):
         cols = slice(low, low + LANES)
         here = pl.ds(pl.multiple_of(step + low, LANES), LANES)
+        there = cols if blocked else here
         lines = slice(low // GROUP, low // GROUP + GROUPS)
-        window = jnp.concatenate([before_ref[:, here] * has_before, prod_ref[:, here]], axis=0)
+        window = jnp.concatenate([before_ref[:, there] * has_before, prod_ref[:, here]], axis=0)
         conv_block(window, fwd_line[lines], 1, (query_ref, cotan_ref), (mixed, grad_query), cols)
-        window = jnp.concatenate([grad_ref[:, here], after_ref[:, here] * has_after], axis=0)
+        window = jnp.concatenate([grad_ref[:, here], after_ref[:, there] * has_after], axis=0)
         conv_block(window, bwd_line[lines], 0, (value_ref, key_ref), (grad_key, grad_value), cols)
 
 
-def gated_convs(keep, taps, turned, prod, before, grad, after, gates, fwd_half, start, count, into):
+def gated_convs(keep, taps, turned, prod, before, grad, after, gates, fwd_half, start, count, blocked, into):
     tok, channels = gates[0].shape
     half = channels // 2 // STEP
     fwd = fwd_half * half + start
@@ -166,18 +167,21 @@
     whole = pl.BlockSpec(memory_space=pltpu.VMEM)
     at_fwd = pl.BlockSpec((tok, STEP), lambda i: (0, fwd + i))
     at_bwd = pl.BlockSpec((tok, STEP), lambda i: (0, bwd + i))
+    halo = pl.BlockSpec((tok, STEP), lambda i: (0, start + i)) if blocked else whole
+    if blocked:
+        before, after = off_chip(before), off_chip(after)
     width = taps.shape[1]
     shape = jax.ShapeDtypeStruct((tok, channels), jnp.bfloat16)
     in_specs = [
         pl.BlockSpec(memory_space=pltpu.SMEM),
-        pl.BlockSpec((STEP // GROUP, width), lambda i: (fwd + i, 0)), whole, whole, at_fwd, at_fwd,
-        pl.BlockSpec((STEP // GROUP, width), lambda i: (bwd + i, 0)), whole, whole, at_bwd, at_bwd,
+        pl.BlockSpec((STEP // GROUP, width), lambda i: (fwd + i, 0)), whole, halo, at_fwd, at_fwd,
+        pl.BlockSpec((STEP // GROUP, width), lambda i: (bwd + i, 0)), whole, halo, at_bwd, at_bwd,
     ]
     query, key, value, cotan = map(off_chip, gates)
     args = [keep, turned, prod, before, query, cotan, taps, grad, after, value, key]
     aliases = {len(args) + n: n for n in range(len(into))}
     return pl.pallas_call(
-        functools.partial(conv_kernel, start * STEP),
+        functools.partial(conv_kernel, start * STEP, blocked),
         grid=(count,),
         in_specs=in_specs + [pl.BlockSpec(memory_space=pl.ANY)] * len(into),
         out_specs=[at_fwd, at_fwd, at_bwd, at_bwd],
@@ -201,10 +205,10 @@
     ortho = jnp.zeros_like(left)
     for i in range(left.shape[0]):
         row = rest[i : i + 1]
-        unit = row / jnp.sqrt(jnp.sum(row * row, axis=1, keepdims=True) + 1e-06)
-        ortho = jnp.where(index == i, unit, ortho)
-        coeff = jnp.sum(left * unit, axis=1, keepdims=True)
-        rest = rest - coeff * unit
+        square = jnp.sum(row * row, axis=1, keepdims=True) + 1e-06
+        coeff = jnp.sum(left * row, axis=1, keepdims=True)
+        ortho = jnp.where(index == i, row / jnp.sqrt(square), ortho)
+        rest = rest - (coeff / square) * row
     right = dot(ortho, grad, NN, HIGH) * scale
     next_ref[...] = right
     low_ref[...] = dot(ortho, right, (((0,), (0,)), ((), ())), HIGH)
@@ -254,8 +258,8 @@
     def beside(start, given, windows, *which):
         nonlocal outs
         got = start(given)
-        windows = tie(*windows, given)[:4]
-        outs = gated_convs(keep, filters, turned, *windows, gates, *which, outs)
+        now, _ = tie(keep, given)
+        outs = gated_convs(now, filters, turned, *windows, gates, *which, outs)
         got, *outs = tie(got, *outs)
         return got
 
@@ -268,16 +272,17 @@
         route = [(i, i ^ distance) for i in range(lax.axis_size("z"))]
         return lambda x: lax.ppermute(x, "z", route)
 
-    piece = beside(exchanged, local, (prod_b, before_b, grad_a, after_a), 1, 0, 2)
-    piece = piece.reshape(count, groups // count, taps).sum(axis=0)
-    grad_b, prod_a, _ = tie(grad_b, prod_a, piece)
+    grad_b, prod_a, local = tie(grad_b, prod_a, local)
     after_b, before_a = from_next(grad_b), from_last(prod_a)
     second = (prod_a, before_a, grad_b, after_b)
-    piece = piece + hop(1)(piece)
+    first = (prod_b, before_b, grad_a, after_a)
+    piece = beside(exchanged, local, first, 1, 0, 1, False)
+    piece = piece.reshape(count, groups // count, taps).sum(axis=0)
+    piece = piece + beside(hop(1), piece, first, 1, 1, 1, False)
     piece = piece + hop(2)(piece)
-    piece = piece + beside(hop(4), piece, second, 0, 0, 1)
+    piece = piece + beside(hop(4), piece, second, 0, 0, 1, True)
     spread = jnp.broadcast_to(piece[None], (count,) + piece.shape).reshape(groups, taps)
-    filter_grad = beside(exchanged, spread, second, 0, 1, 1)
+    filter_grad = beside(exchanged, spread, second, 0, 1, 1, True)
     scale = (lax.axis_size("dp") * size * tok * (channels // groups)) ** (-0.5)
     low, right = low_rank(filter_grad, basis_prev.T, scale)
     return (*[out[None] for out in outs], low, right.T)

time: 83.5 us -> 78.3 us (0.938)
  starting transfers between devices: 33.6 us -> 30.2 us
  waiting for transfers between devices: 17.2 us -> 14.5 us
  Pallas kernels: 30.5 us -> 31.4 us
    all_to_all x2, starting transfers between devices: 28.3 us -> 23.4 us  [exchanged(): return lax.all_to_all(x, near, 0, 0, tiled=True)]
    ppermute x3, waiting for transfers between devices: 6.22 us -> 3.75 us  [hop(): return lambda x: lax.ppermute(x, 'z', route)]
    pallas_call x3 -> x4, Pallas kernels: 15.7 us -> 17.9 us  [gated_convs(): pl.pallas_call(functools.partial(conv_kernel, start * STEP, blocked), gri...]
    ppermute x2, waiting for transfers between devices: 5.82 us -> 4.21 us  [from_next(): return lax.ppermute(x, seq, [(i, (i - 1) % size) for i in range(size)])]
    all_to_all x2, waiting for transfers between devices: 4.1 us -> 5.44 us  [exchanged(): return lax.all_to_all(x, near, 0, 0, tiled=True)]
    pallas_call x1, Pallas kernels: 4.15 us -> 2.88 us  [low_rank(): pl.pallas_call(functools.partial(low_rank_kernel, scale), out_shape=[jax....]
  transfers between devices with their start and end apart: 9 -> 9, of which waited for: 7 -> 6; matrix products, arithmetic and copies ran while one was open for 0% -> 0% of each run, Pallas kernels for 21% -> 25%
where the time goes in v1:
time: 78.3 us; the launch traced here: 77.8 us
  Pallas kernels  31.4 us (40%)
  starting transfers between devices  30.2 us (39%)
  waiting for transfers between devices  14.5 us (19%)
  local copies, waits for them, and re-layouts  0.9 us (1%)
    all_to_all x2, starting transfers between devices, exchanged(): return lax.all_to_all(x, near, 0, 0, tiled=True)  23.4 us
    pallas_call x4, Pallas kernels, gated_convs(): pl.pallas_call(functools.partial(conv_kernel, start * STEP, blocked), gri...  17.9 us
    pallas_call x1, Pallas kernels, lag_sums(): pl.pallas_call(lag_kernel, in_specs=[pl.BlockSpec(memory_space=pltpu.SMEM...  7.14 us
    all_to_all x2, waiting for transfers between devices, exchanged(): return lax.all_to_all(x, near, 0, 0, tiled=True)  5.44 us
    ppermute x2, waiting for transfers between devices, from_next(): return lax.ppermute(x, seq, [(i, (i - 1) % size) for i in range(size)])  4.21 us
    ppermute x3, waiting for transfers between devices, hop(): return lambda x: lax.ppermute(x, 'z', route)  3.75 us
    pallas_call x2, Pallas kernels, gated(): pl.pallas_call(gate_kernel, grid=(steps,), in_specs=[grad_at, grad_at, pr...  3.46 us
    ppermute x2, starting transfers between devices, from_next(): return lax.ppermute(x, seq, [(i, (i - 1) % size) for i in range(size)])  3.32 us
  transfers between devices with their start and end apart: 9, of which 6 were waited for; matrix products, arithmetic and copies ran while one was open for 0% of the time, Pallas kernels for 25%

profile of v1, /device:TPU:1, one launch (start us, length us, event | category | flops | bytes accessed | tf_op | source)
XLA Modules:
  0.0 77.8 jit_solution(4416472383439652235)
XLA Ops:
  0.6 0.0 copy-start
  0.6 1.7 %gated.2 = (bf16[128,2048]{1,0:T(8,128)(2,1)S(1)}, bf16[128,2048]{1,0:T(8,128)(2,1)S(1)}) custom-call(bf16[128,4096]{1,0:T(8,128)(2,1)} %bitcast.19, bf16[128,4096]{1,0:T(8,128)(2,1)} %bitcast.25, bf16[128,4096]{1,0:T(8,128)(2,1)} %bitcast.31, bf16[128,4096]{1,0:T(8,128)(2,1)} %bitcast.37), custom_call_target="tpu_custom_call" | custom-call | flops 524288 | bytes 3145728 | tf_op jit(solution)/shard_map/gated/pallas_call | solution.py:45
  2.4 3.3 %collective-permute-start = (bf16[128,2048]{1,0:T(8,128)(2,1)S(1)}, bf16[128,2048]{1,0:T(8,128)(2,1)S(1)}, u32[]{:S(2)}, u32[]{:S(2)}) collective-permute-start(bf16[128,2048]{1,0:T(8,128)(2,1)S(1)} %get-tuple-element.58.grad_a.grad_ref), channel_id=1, source_target_pairs={{0,63},{1,0},{2,1},{3,2},{4,3},{5,4},{6,5},{7,6},{8,7},{9,8},{10,9... | collective-permute-start | bytes 1572872 | tf_op jit(solution)/shard_map/ppermute | solution.py:243
  5.7 0.0 collective-permute-start.1
  5.7 0.0 copy-done
  5.7 0.2 rev.3.fwd_line
  5.9 0.0 copy-start.2
  5.9 0.0 copy-start.3
  5.9 0.0 copy-start.4
  5.9 1.8 %gated.3 = (bf16[128,2048]{1,0:T(8,128)(2,1)S(1)}, bf16[128,2048]{1,0:T(8,128)(2,1)S(1)}) custom-call(bf16[128,4096]{1,0:T(8,128)(2,1)} %bitcast.20, bf16[128,4096]{1,0:T(8,128)(2,1)} %bitcast.26, bf16[128,4096]{1,0:T(8,128)(2,1)} %bitcast.32, bf16[128,4096]{1,0:T(8,128)(2,1)} %bitcast.38), custom_call_target="tpu_custom_call" | custom-call | flops 524288 | bytes 3145728 | tf_op jit(solution)/shard_map/gated/pallas_call | solution.py:45
  7.7 0.1 add_convert_fusion.keep_ref
  7.8 4.2 %collective-permute-done.after_ref = bf16[128,2048]{1,0:T(8,128)(2,1)S(1)} collective-permute-done((bf16[128,2048]{1,0:T(8,128)(2,1)S(1)}, bf16[128,2048]{1,0:T(8,128)(2,1)S(1)}, u32[]{:S(2)}, u32[]{:S(2)}) %collective-permute-start) | collective-permute-done | bytes 524320 | tf_op jit(solution)/shard_map/ppermute | solution.py:243
  12.0 1.1 %collective-permute-done.1.before_ref = bf16[128,2048]{1,0:T(8,128)(2,1)S(1)} collective-permute-done((bf16[128,2048]{1,0:T(8,128)(2,1)S(1)}, bf16[128,2048]{1,0:T(8,128)(2,1)S(1)}, u32[]{:S(2)}, u32[]{:S(2)}) %collective-permute-start.1) | collective-permute-done | bytes 524320 | tf_op jit(solution)/shard_map/ppermute | solution.py:246
  13.1 0.0 copy-done.2
  13.1 0.0 copy-done.3
  13.1 0.0 copy-done.4
  13.1 7.1 %lag_sums.1 = f32[256,128]{1,0:T(8,128)} custom-call(f32[2]{0:T(128)S(1)} %add_convert_fusion.keep_ref, bf16[128,2048]{1,0:T(8,128)(2,1)S(1)} %get-tuple-element.84.prod_a.prod_ref, bf16[128,2048]{1,0:T(8,128)(2,1)S(1)} %get-tuple-element.58.grad_a.grad_ref, bf16[128,2048]{1,0:T(8,128)(2,1)S(1)} %collective-permute-done.after_ref, ...), custom_call_target="tpu_custom_call" | custom-call | flops 4294967296 | bytes 3145728 | tf_op jit(solution)/shard_map/lag_sums/pallas_call | solution.py:104
  20.2 15.0 %all-to-all-start = ((f32[32,8,128]{2,1,0:T(8,128)}), f32[32,8,128]{2,1,0:T(8,128)S(1)}, u32[]{:S(2)}, u32[]{:S(2)}) async-start(f32[32,8,128]{2,1,0:T(8,128)} %bitcast.6), calls=%async_computation | async-start | bytes 262144 | tf_op jit(solution)/shard_map/all_to_all | solution.py:269
  35.2 1.7 %collective-permute-start.5 = (bf16[128,2048]{1,0:T(8,128)(2,1)S(1)}, bf16[128,2048]{1,0:T(8,128)(2,1)}, u32[]{:S(2)}, u32[]{:S(2)}) collective-permute-start(bf16[128,2048]{1,0:T(8,128)(2,1)S(1)} %get-tuple-element.84.prod_a.prod_ref), channel_id=1, source_target_pairs={{0,1},{1,2},{2,3},{3,4},{4,5},{5,6},{6,7},{7,8},{8,9},{9,10},{10,1... | collective-permute-start | bytes 1572872 | tf_op jit(solution)/shard_map/ppermute | solution.py:246
  36.9 0.0 collective-permute-start.6
  36.9 4.4 %gated_convs.4 = (bf16[128,4096]{1,0:T(8,128)(2,1)}, bf16[128,4096]{1,0:T(8,128)(2,1)}, bf16[128,4096]{1,0:T(8,128)(2,1)}, bf16[128,4096]{1,0:T(8,128)(2,1)}) custom-call(f32[2]{0:T(128)S(1)} %add_convert_fusion.keep_ref, bf16[256,128]{1,0:T(8,128)(2,1)S(1)} %rev.3.fwd_line, bf16[128,2048]{1,0:T(8,128)(2,1)S(1)} %get-tuple-element.59.prod_b.prod_ref, ...), custom_call_target="tpu_custom_call" | custom-call | flops 4294967296 | bytes 3145728 | tf_op jit(solution)/shard_map/gated_convs/pallas_call | solution.py:183
  41.3 2.3 %all-to-all-done = f32[32,8,128]{2,1,0:T(8,128)S(1)} async-done(((f32[32,8,128]{2,1,0:T(8,128)}), f32[32,8,128]{2,1,0:T(8,128)S(1)}, u32[]{:S(2)}, u32[]{:S(2)}) %all-to-all-start) | async-done | bytes 131104 | tf_op jit(solution)/shard_map/all_to_all | solution.py:269
  43.7 0.3 collective-permute-start.2
  43.9 4.4 %gated_convs.5 = (bf16[128,4096]{1,0:T(8,128)(2,1)}, bf16[128,4096]{1,0:T(8,128)(2,1)}, bf16[128,4096]{1,0:T(8,128)(2,1)}, bf16[128,4096]{1,0:T(8,128)(2,1)}) custom-call(f32[2]{0:T(128)S(1)} %add_convert_fusion.keep_ref, bf16[256,128]{1,0:T(8,128)(2,1)S(1)} %rev.3.fwd_line, ...), custom_call_target="tpu_custom_call", output_to_operand_aliasing={{0}: (11, {}), {1}: (12, {}), {2}: (13, {}), {3}: (14, {})} | custom-call | flops 4294967296 | bytes 3145728 | tf_op jit(solution)/shard_map/gated_convs/pallas_call | solution.py:183
  48.4 0.0 collective-permute-done.2
  48.4 0.1 collective-permute-start.3
  48.5 3.3 %collective-permute-done.3 = f32[8,128]{1,0:T(8,128)S(1)} collective-permute-done((f32[8,128]{1,0:T(8,128)S(1)}, f32[8,128]{1,0:T(8,128)S(1)}, u32[]{:S(2)}, u32[]{:S(2)}) %collective-permute-start.3) | collective-permute-done | bytes 4128 | tf_op jit(solution)/shard_map/ppermute | solution.py:273
  51.8 1.4 %collective-permute-start.4 = (f32[8,128]{1,0:T(8,128)S(1)}, f32[8,128]{1,0:T(8,128)S(1)}, u32[]{:S(2)}, u32[]{:S(2)}) collective-permute-start(f32[8,128]{1,0:T(8,128)S(1)} %add.18), channel_id=1, source_target_pairs={{0,32},{8,40},{16,48},{24,56},{32,0},{40,8},{48,16},{56,24},{1,33}... | collective-permute-start | bytes 12296 | tf_op jit(solution)/shard_map/ppermute | solution.py:273
  53.2 0.0 collective-permute-done.5.before_ref
  53.2 0.0 collective-permute-done.6.after_ref
  53.2 4.6 %gated_convs.6 = (bf16[128,4096]{1,0:T(8,128)(2,1)}, bf16[128,4096]{1,0:T(8,128)(2,1)}, bf16[128,4096]{1,0:T(8,128)(2,1)}, bf16[128,4096]{1,0:T(8,128)(2,1)}) custom-call(f32[2]{0:T(128)S(1)} %add_convert_fusion.keep_ref, bf16[256,128]{1,0:T(8,128)(2,1)S(1)} %rev.3.fwd_line, ...), custom_call_target="tpu_custom_call", output_to_operand_aliasing={{0}: (11, {}), {1}: (12, {}), {2}: (13, {}), {3}: (14, {})} | custom-call | flops 4294967296 | bytes 3145728 | tf_op jit(solution)/shard_map/gated_convs/pallas_call | solution.py:183
  57.8 0.4 collective-permute-done.4
  58.2 0.7 broadcast_in_dim.18
  58.8 8.4 %all-to-all-start.1 = ((f32[32,8,128]{2,1,0:T(8,128)}), f32[32,8,128]{2,1,0:T(8,128)S(1)}, u32[]{:S(2)}, u32[]{:S(2)}) async-start(f32[32,8,128]{2,1,0:T(8,128)} %broadcast_in_dim.18), calls=%async_computation.1 | async-start | bytes 262144 | tf_op jit(solution)/shard_map/all_to_all | solution.py:269
  67.3 4.6 %gated_convs.7 = (bf16[128,4096]{1,0:T(8,128)(2,1)}, bf16[128,4096]{1,0:T(8,128)(2,1)}, bf16[128,4096]{1,0:T(8,128)(2,1)}, bf16[128,4096]{1,0:T(8,128)(2,1)}) custom-call(f32[2]{0:T(128)S(1)} %add_convert_fusion.keep_ref, bf16[256,128]{1,0:T(8,128)(2,1)S(1)} %rev.3.fwd_line, ...), custom_call_target="tpu_custom_call", output_to_operand_aliasing={{0}: (11, {}), {1}: (12, {}), {2}: (13, {}), {3}: (14, {})} | custom-call | flops 4294967296 | bytes 3145728 | tf_op jit(solution)/shard_map/gated_convs/pallas_call | solution.py:183
  71.8 0.0 copy-start.1
  71.8 3.1 %all-to-all-done.1 = f32[32,8,128]{2,1,0:T(8,128)S(1)} async-done(((f32[32,8,128]{2,1,0:T(8,128)}), f32[32,8,128]{2,1,0:T(8,128)S(1)}, u32[]{:S(2)}, u32[]{:S(2)}) %all-to-all-start.1) | async-done | bytes 131104 | tf_op jit(solution)/shard_map/all_to_all | solution.py:269
  75.0 0.0 copy-done.1
  75.0 2.9 %low_rank.1 = (f32[256,128]{1,0:T(8,128)}, f32[16,128]{1,0:T(8,128)}) custom-call(f32[256,128]{1,0:T(8,128)S(1)} %bitcast.17, f32[16,128]{1,0:T(8,128)S(1)} %bitcast.18), custom_call_target="tpu_custom_call" | custom-call | tf_op jit(solution)/shard_map/low_rank/pallas_call | solution.py:218
  (4 shorter events, 0.0 us)
Async XLA Ops:
  0.6 5.0 %copy-start = (bf16[256,128]{1,0:T(8,128)(2,1)S(1)}, bf16[256,128]{1,0:T(8,128)(2,1)}, u32[]{:S(2)}) copy-start(bf16[256,128]{1,0:T(8,128)(2,1)} %bwd_line.7) | copy-start | bytes 196612
  2.4 9.6 %collective-permute-start = (bf16[128,2048]{1,0:T(8,128)(2,1)S(1)}, bf16[128,2048]{1,0:T(8,128)(2,1)S(1)}, u32[]{:S(2)}, u32[]{:S(2)}) collective-permute-start(bf16[128,2048]{1,0:T(8,128)(2,1)S(1)} %get-tuple-element.58.grad_a.grad_ref), channel_id=1, source_target_pairs={{0,63},{1,0},{2,1},{3,2},{4,3},{5,4},{6,5},{7,6},{8,7},{9,8},{10,9... | collective-permute-start | bytes 1572872 | tf_op jit(solution)/shard_map/ppermute | solution.py:243
  5.7 7.4 %collective-permute-start.1 = (bf16[128,2048]{1,0:T(8,128)(2,1)S(1)}, bf16[128,2048]{1,0:T(8,128)(2,1)S(1)}, u32[]{:S(2)}, u32[]{:S(2)}) collective-permute-start(bf16[128,2048]{1,0:T(8,128)(2,1)S(1)} %get-tuple-element.59.prod_b.prod_ref), channel_id=1, source_target_pairs={{0,1},{1,2},{2,3},{3,4},{4,5},{5,6},{6,7},{7,8},{8,9},{9,10},{10,1... | collective-permute-start | bytes 1572872 | tf_op jit(solution)/shard_map/ppermute | solution.py:246
  5.9 7.2 %copy-start.2 = (bf16[256,256]{1,0:T(8,128)(2,1)S(1)}, bf16[256,256]{1,0:T(8,128)(2,1)}, u32[]{:S(2)}) copy-start(bf16[256,256]{1,0:T(8,128)(2,1)} %constant.28.clone.mask_ref) | copy-start | bytes 393220
  5.9 7.2 %copy-start.3 = (f32[256,128]{1,0:T(8,128)S(1)}, f32[256,128]{1,0:T(8,128)}, u32[]{:S(2)}) copy-start(f32[256,128]{1,0:T(8,128)} %constant.30.clone.turn_ref) | copy-start | bytes 393220
  5.9 7.2 %copy-start.4 = (bf16[128,128]{1,0:T(8,128)(2,1)S(1)}, bf16[128,128]{1,0:T(8,128)(2,1)}, u32[]{:S(2)}) copy-start(bf16[128,128]{1,0:T(8,128)(2,1)} %constant.29.clone.flip_ref) | copy-start | bytes 98308
  20.2 23.4 %all-to-all-start = ((f32[32,8,128]{2,1,0:T(8,128)}), f32[32,8,128]{2,1,0:T(8,128)S(1)}, u32[]{:S(2)}, u32[]{:S(2)}) async-start(f32[32,8,128]{2,1,0:T(8,128)} %bitcast.6), calls=%async_computation | async-start | bytes 262144 | tf_op jit(solution)/shard_map/all_to_all | solution.py:269
  35.2 18.0 %collective-permute-start.5 = (bf16[128,2048]{1,0:T(8,128)(2,1)S(1)}, bf16[128,2048]{1,0:T(8,128)(2,1)}, u32[]{:S(2)}, u32[]{:S(2)}) collective-permute-start(bf16[128,2048]{1,0:T(8,128)(2,1)S(1)} %get-tuple-element.84.prod_a.prod_ref), channel_id=1, source_target_pairs={{0,1},{1,2},{2,3},{3,4},{4,5},{5,6},{6,7},{7,8},{8,9},{9,10},{10,1... | collective-permute-start | bytes 1572872 | tf_op jit(solution)/shard_map/ppermute | solution.py:246
  36.9 16.3 %collective-permute-start.6 = (bf16[128,2048]{1,0:T(8,128)(2,1)S(1)}, bf16[128,2048]{1,0:T(8,128)(2,1)}, u32[]{:S(2)}, u32[]{:S(2)}) collective-permute-start(bf16[128,2048]{1,0:T(8,128)(2,1)S(1)} %get-tuple-element.85.grad_b.grad_ref), channel_id=1, source_target_pairs={{0,63},{1,0},{2,1},{3,2},{4,3},{5,4},{6,5},{7,6},{8,7},{9,8},{10,9... | collective-permute-start | bytes 1572872 | tf_op jit(solution)/shard_map/ppermute | solution.py:243
  43.7 4.7 %collective-permute-start.2 = (f32[8,128]{1,0:T(8,128)S(1)}, f32[8,128]{1,0:T(8,128)S(1)}, u32[]{:S(2)}, u32[]{:S(2)}) collective-permute-start(f32[8,128]{1,0:T(8,128)S(1)} %bitcast_reduce_fusion), channel_id=1, source_target_pairs={{0,8},{8,0},{16,24},{24,16},{32,40},{40,32},{48,56},{56,48},{1,9},... | collective-permute-start | bytes 12296 | tf_op jit(solution)/shard_map/ppermute | solution.py:273
  48.4 3.4 %collective-permute-start.3 = (f32[8,128]{1,0:T(8,128)S(1)}, f32[8,128]{1,0:T(8,128)S(1)}, u32[]{:S(2)}, u32[]{:S(2)}) collective-permute-start(f32[8,128]{1,0:T(8,128)S(1)} %add.17), channel_id=1, source_target_pairs={{0,16},{8,24},{16,0},{24,8},{32,48},{40,56},{48,32},{56,40},{1,17}... | collective-permute-start | bytes 12296 | tf_op jit(solution)/shard_map/ppermute | solution.py:273
  51.8 6.4 %collective-permute-start.4 = (f32[8,128]{1,0:T(8,128)S(1)}, f32[8,128]{1,0:T(8,128)S(1)}, u32[]{:S(2)}, u32[]{:S(2)}) collective-permute-start(f32[8,128]{1,0:T(8,128)S(1)} %add.18), channel_id=1, source_target_pairs={{0,32},{8,40},{16,48},{24,56},{32,0},{40,8},{48,16},{56,24},{1,33}... | collective-permute-start | bytes 12296 | tf_op jit(solution)/shard_map/ppermute | solution.py:273
  58.8 16.1 %all-to-all-start.1 = ((f32[32,8,128]{2,1,0:T(8,128)}), f32[32,8,128]{2,1,0:T(8,128)S(1)}, u32[]{:S(2)}, u32[]{:S(2)}) async-start(f32[32,8,128]{2,1,0:T(8,128)} %broadcast_in_dim.18), calls=%async_computation.1 | async-start | bytes 262144 | tf_op jit(solution)/shard_map/all_to_all | solution.py:269
  71.8 3.1 %copy-start.1 = (f32[128,16]{0,1:T(8,128)S(1)}, f32[128,16]{0,1:T(8,128)}, u32[]{:S(2)}) copy-start(f32[128,16]{0,1:T(8,128)} %param.14) | copy-start | bytes 24580

commit v2 on v1

--- a/solution.py
+++ b/solution.py
@@ -70,7 +70,7 @@
 
 
 def lag_kernel(
-    keep_ref, prod_a, grad_a, after_ref, prod_b, grad_b, before_ref, mask_ref, flip_ref, turn_ref, out_ref
+    keep_ref, prod_b, grad_b, before_ref, prod_a, grad_a, after_ref, mask_ref, flip_ref, turn_ref, out_ref
 ):
     taps = out_ref.shape[1]
     has_before = keep_ref[0].astype(jnp.bfloat16)
@@ -113,7 +113,7 @@
             transcendentals=0,
         ),
         name="lag_sums",
-    )(keep, prod_a, grad_a, after, prod_b, grad_b, before, *fixed)
+    )(keep, prod_b, grad_b, before, prod_a, grad_a, after, *fixed)
 
 
 def conv_block(window, line, shift, gates, outs, cols):

time: 78.3 us -> 76.8 us (0.981)
  waiting for transfers between devices: 14.5 us -> 11.9 us
  starting transfers between devices: 30.2 us -> 31.3 us
    ppermute x3, starting transfers between devices: 1.76 us -> 9.84 us  [hop(): return lambda x: lax.ppermute(x, 'z', route)]
    all_to_all x2, starting transfers between devices: 23.4 us -> 16.4 us  [exchanged(): return lax.all_to_all(x, near, 0, 0, tiled=True)]
    ppermute x2, starting transfers between devices: 1.71 us -> 4.47 us  [from_last(): return lax.ppermute(x, seq, [(i, (i + 1) % size) for i in range(size)])]
    ppermute x3, waiting for transfers between devices: 3.75 us -> 1 us  [hop(): return lambda x: lax.ppermute(x, 'z', route)]
    ppermute x2, starting transfers between devices: 3.32 us -> 0.65 us  [from_next(): return lax.ppermute(x, seq, [(i, (i - 1) % size) for i in range(size)])]
    ppermute x2, waiting for transfers between devices: 1.1 us -> 3.4 us  [from_last(): return lax.ppermute(x, seq, [(i, (i + 1) % size) for i in range(size)])]
    ppermute x2, waiting for transfers between devices: 4.21 us -> 2.78 us  [from_next(): return lax.ppermute(x, seq, [(i, (i - 1) % size) for i in range(size)])]
  transfers between devices with their start and end apart: 9 -> 9, of which waited for: 6 -> 5; matrix products, arithmetic and copies ran while one was open for 0% -> 0% of each run, Pallas kernels for 25% -> 26%
where the time goes in v2:
time: 76.8 us; the launch traced here: 76.4 us
  Pallas kernels  31.4 us (41%)
  starting transfers between devices  31.3 us (41%)
  waiting for transfers between devices  11.9 us (15%)
  local copies, waits for them, and re-layouts  0.89 us (1%)
    pallas_call x4, Pallas kernels, gated_convs(): pl.pallas_call(functools.partial(conv_kernel, start * STEP, blocked), gri...  17.9 us
    all_to_all x2, starting transfers between devices, exchanged(): return lax.all_to_all(x, near, 0, 0, tiled=True)  16.4 us
    ppermute x3, starting transfers between devices, hop(): return lambda x: lax.ppermute(x, 'z', route)  9.84 us
    pallas_call x1, Pallas kernels, lag_sums(): pl.pallas_call(lag_kernel, in_specs=[pl.BlockSpec(memory_space=pltpu.SMEM...  7.15 us
    all_to_all x2, waiting for transfers between devices, exchanged(): return lax.all_to_all(x, near, 0, 0, tiled=True)  4.74 us
    ppermute x2, starting transfers between devices, from_last(): return lax.ppermute(x, seq, [(i, (i + 1) % size) for i in range(size)])  4.47 us
    pallas_call x2, Pallas kernels, gated(): pl.pallas_call(gate_kernel, grid=(steps,), in_specs=[grad_at, grad_at, pr...  3.46 us
    ppermute x2, waiting for transfers between devices, from_last(): return lax.ppermute(x, seq, [(i, (i + 1) % size) for i in range(size)])  3.4 us
  transfers between devices with their start and end apart: 9, of which 5 were waited for; matrix products, arithmetic and copies ran while one was open for 0% of the time, Pallas kernels for 26%

profile of v2, /device:TPU:1, one launch (start us, length us, event | category | flops | bytes accessed | tf_op | source)
XLA Modules:
  0.0 76.4 jit_solution(17228145474956148163)
XLA Ops:
  0.6 0.0 copy-start
  0.6 1.7 %gated.2 = (bf16[128,2048]{1,0:T(8,128)(2,1)S(1)}, bf16[128,2048]{1,0:T(8,128)(2,1)S(1)}) custom-call(bf16[128,4096]{1,0:T(8,128)(2,1)} %bitcast.19, bf16[128,4096]{1,0:T(8,128)(2,1)} %bitcast.25, bf16[128,4096]{1,0:T(8,128)(2,1)} %bitcast.31, bf16[128,4096]{1,0:T(8,128)(2,1)} %bitcast.37), custom_call_target="tpu_custom_call" | custom-call | flops 524288 | bytes 3145728 | tf_op jit(solution)/shard_map/gated/pallas_call | solution.py:45
  2.4 2.8 %collective-permute-start = (bf16[128,2048]{1,0:T(8,128)(2,1)S(1)}, bf16[128,2048]{1,0:T(8,128)(2,1)S(1)}, u32[]{:S(2)}, u32[]{:S(2)}) collective-permute-start(bf16[128,2048]{1,0:T(8,128)(2,1)S(1)} %get-tuple-element.59.prod_b.prod_ref), channel_id=1, source_target_pairs={{0,1},{1,2},{2,3},{3,4},{4,5},{5,6},{6,7},{7,8},{8,9},{9,10},{10,1... | collective-permute-start | bytes 1572872 | tf_op jit(solution)/shard_map/ppermute | solution.py:246
  5.1 0.6 collective-permute-start.1
  5.8 0.0 copy-done
  5.8 0.2 rev.3.fwd_line
  6.0 0.0 copy-start.2
  6.0 0.0 copy-start.3
  6.0 0.0 copy-start.4
  6.0 1.8 %gated.3 = (bf16[128,2048]{1,0:T(8,128)(2,1)S(1)}, bf16[128,2048]{1,0:T(8,128)(2,1)S(1)}) custom-call(bf16[128,4096]{1,0:T(8,128)(2,1)} %bitcast.20, bf16[128,4096]{1,0:T(8,128)(2,1)} %bitcast.26, bf16[128,4096]{1,0:T(8,128)(2,1)} %bitcast.32, bf16[128,4096]{1,0:T(8,128)(2,1)} %bitcast.38), custom_call_target="tpu_custom_call" | custom-call | flops 524288 | bytes 3145728 | tf_op jit(solution)/shard_map/gated/pallas_call | solution.py:45
  7.8 0.1 add_convert_fusion.keep_ref
  7.9 3.4 %collective-permute-done.before_ref = bf16[128,2048]{1,0:T(8,128)(2,1)S(1)} collective-permute-done((bf16[128,2048]{1,0:T(8,128)(2,1)S(1)}, bf16[128,2048]{1,0:T(8,128)(2,1)S(1)}, u32[]{:S(2)}, u32[]{:S(2)}) %collective-permute-start) | collective-permute-done | bytes 524320 | tf_op jit(solution)/shard_map/ppermute | solution.py:246
  11.2 2.8 %collective-permute-done.1.after_ref = bf16[128,2048]{1,0:T(8,128)(2,1)S(1)} collective-permute-done((bf16[128,2048]{1,0:T(8,128)(2,1)S(1)}, bf16[128,2048]{1,0:T(8,128)(2,1)S(1)}, u32[]{:S(2)}, u32[]{:S(2)}) %collective-permute-start.1) | collective-permute-done | bytes 524320 | tf_op jit(solution)/shard_map/ppermute | solution.py:243
  14.0 0.0 copy-done.2
  14.0 0.0 copy-done.3
  14.0 0.0 copy-done.4
  14.0 7.1 %lag_sums.1 = f32[256,128]{1,0:T(8,128)} custom-call(f32[2]{0:T(128)S(1)} %add_convert_fusion.keep_ref, bf16[128,2048]{1,0:T(8,128)(2,1)S(1)} %get-tuple-element.59.prod_b.prod_ref, bf16[128,2048]{1,0:T(8,128)(2,1)S(1)} %get-tuple-element.85.grad_b.grad_ref, bf16[128,2048]{1,0:T(8,128)(2,1)S(1)} %collective-permute-done.before_ref, ...), custom_call_target="tpu_custom_call" | custom-call | flops 4294967296 | bytes 3145728 | tf_op jit(solution)/shard_map/lag_sums/pallas_call | solution.py:104
  21.2 9.0 %all-to-all-start = ((f32[32,8,128]{2,1,0:T(8,128)}), f32[32,8,128]{2,1,0:T(8,128)S(1)}, u32[]{:S(2)}, u32[]{:S(2)}) async-start(f32[32,8,128]{2,1,0:T(8,128)} %bitcast.6), calls=%async_computation | async-start | bytes 262144 | tf_op jit(solution)/shard_map/all_to_all | solution.py:269
  30.2 1.7 %collective-permute-start.5 = (bf16[128,2048]{1,0:T(8,128)(2,1)S(1)}, bf16[128,2048]{1,0:T(8,128)(2,1)}, u32[]{:S(2)}, u32[]{:S(2)}) collective-permute-start(bf16[128,2048]{1,0:T(8,128)(2,1)S(1)} %get-tuple-element.84.prod_a.prod_ref), channel_id=1, source_target_pairs={{0,1},{1,2},{2,3},{3,4},{4,5},{5,6},{6,7},{7,8},{8,9},{9,10},{10,1... | collective-permute-start | bytes 1572872 | tf_op jit(solution)/shard_map/ppermute | solution.py:246
  31.9 0.0 collective-permute-start.6
  31.9 4.4 %gated_convs.4 = (bf16[128,4096]{1,0:T(8,128)(2,1)}, bf16[128,4096]{1,0:T(8,128)(2,1)}, bf16[128,4096]{1,0:T(8,128)(2,1)}, bf16[128,4096]{1,0:T(8,128)(2,1)}) custom-call(f32[2]{0:T(128)S(1)} %add_convert_fusion.keep_ref, bf16[256,128]{1,0:T(8,128)(2,1)S(1)} %rev.3.fwd_line, bf16[128,2048]{1,0:T(8,128)(2,1)S(1)} %get-tuple-element.59.prod_b.prod_ref, ...), custom_call_target="tpu_custom_call" | custom-call | flops 4294967296 | bytes 3145728 | tf_op jit(solution)/shard_map/gated_convs/pallas_call | solution.py:183
  36.3 1.6 %all-to-all-done = f32[32,8,128]{2,1,0:T(8,128)S(1)} async-done(((f32[32,8,128]{2,1,0:T(8,128)}), f32[32,8,128]{2,1,0:T(8,128)S(1)}, u32[]{:S(2)}, u32[]{:S(2)}) %all-to-all-start) | async-done | bytes 131104 | tf_op jit(solution)/shard_map/all_to_all | solution.py:269
  37.9 2.3 %collective-permute-start.2 = (f32[8,128]{1,0:T(8,128)S(1)}, f32[8,128]{1,0:T(8,128)S(1)}, u32[]{:S(2)}, u32[]{:S(2)}) collective-permute-start(f32[8,128]{1,0:T(8,128)S(1)} %bitcast_reduce_fusion), channel_id=1, source_target_pairs={{0,8},{8,0},{16,24},{24,16},{32,40},{40,32},{48,56},{56,48},{1,9},... | collective-permute-start | bytes 12296 | tf_op jit(solution)/shard_map/ppermute | solution.py:273
  40.2 4.4 %gated_convs.5 = (bf16[128,4096]{1,0:T(8,128)(2,1)}, bf16[128,4096]{1,0:T(8,128)(2,1)}, bf16[128,4096]{1,0:T(8,128)(2,1)}, bf16[128,4096]{1,0:T(8,128)(2,1)}) custom-call(f32[2]{0:T(128)S(1)} %add_convert_fusion.keep_ref, bf16[256,128]{1,0:T(8,128)(2,1)S(1)} %rev.3.fwd_line, ...), custom_call_target="tpu_custom_call", output_to_operand_aliasing={{0}: (11, {}), {1}: (12, {}), {2}: (13, {}), {3}: (14, {})} | custom-call | flops 4294967296 | bytes 3145728 | tf_op jit(solution)/shard_map/gated_convs/pallas_call | solution.py:183
  44.6 0.0 collective-permute-done.2
  44.6 5.5 %collective-permute-start.3 = (f32[8,128]{1,0:T(8,128)S(1)}, f32[8,128]{1,0:T(8,128)S(1)}, u32[]{:S(2)}, u32[]{:S(2)}) collective-permute-start(f32[8,128]{1,0:T(8,128)S(1)} %add.17), channel_id=1, source_target_pairs={{0,16},{8,24},{16,0},{24,8},{32,48},{40,56},{48,32},{56,40},{1,17}... | collective-permute-start | bytes 12296 | tf_op jit(solution)/shard_map/ppermute | solution.py:273
  50.1 1.0 %collective-permute-done.3 = f32[8,128]{1,0:T(8,128)S(1)} collective-permute-done((f32[8,128]{1,0:T(8,128)S(1)}, f32[8,128]{1,0:T(8,128)S(1)}, u32[]{:S(2)}, u32[]{:S(2)}) %collective-permute-start.3) | collective-permute-done | bytes 4128 | tf_op jit(solution)/shard_map/ppermute | solution.py:273
  51.1 2.1 %collective-permute-start.4 = (f32[8,128]{1,0:T(8,128)S(1)}, f32[8,128]{1,0:T(8,128)S(1)}, u32[]{:S(2)}, u32[]{:S(2)}) collective-permute-start(f32[8,128]{1,0:T(8,128)S(1)} %add.18), channel_id=1, source_target_pairs={{0,32},{8,40},{16,48},{24,56},{32,0},{40,8},{48,16},{56,24},{1,33}... | collective-permute-start | bytes 12296 | tf_op jit(solution)/shard_map/ppermute | solution.py:273
  53.2 0.0 collective-permute-done.5.before_ref
  53.2 0.0 collective-permute-done.6.after_ref
  53.2 4.6 %gated_convs.6 = (bf16[128,4096]{1,0:T(8,128)(2,1)}, bf16[128,4096]{1,0:T(8,128)(2,1)}, bf16[128,4096]{1,0:T(8,128)(2,1)}, bf16[128,4096]{1,0:T(8,128)(2,1)}) custom-call(f32[2]{0:T(128)S(1)} %add_convert_fusion.keep_ref, bf16[256,128]{1,0:T(8,128)(2,1)S(1)} %rev.3.fwd_line, ...), custom_call_target="tpu_custom_call", output_to_operand_aliasing={{0}: (11, {}), {1}: (12, {}), {2}: (13, {}), {3}: (14, {})} | custom-call | flops 4294967296 | bytes 3145728 | tf_op jit(solution)/shard_map/gated_convs/pallas_call | solution.py:183
  57.7 0.0 collective-permute-done.4
  57.7 0.7 broadcast_in_dim.18
  58.4 7.4 %all-to-all-start.1 = ((f32[32,8,128]{2,1,0:T(8,128)}), f32[32,8,128]{2,1,0:T(8,128)S(1)}, u32[]{:S(2)}, u32[]{:S(2)}) async-start(f32[32,8,128]{2,1,0:T(8,128)} %broadcast_in_dim.18), calls=%async_computation.1 | async-start | bytes 262144 | tf_op jit(solution)/shard_map/all_to_all | solution.py:269
  65.8 4.6 %gated_convs.7 = (bf16[128,4096]{1,0:T(8,128)(2,1)}, bf16[128,4096]{1,0:T(8,128)(2,1)}, bf16[128,4096]{1,0:T(8,128)(2,1)}, bf16[128,4096]{1,0:T(8,128)(2,1)}) custom-call(f32[2]{0:T(128)S(1)} %add_convert_fusion.keep_ref, bf16[256,128]{1,0:T(8,128)(2,1)S(1)} %rev.3.fwd_line, ...), custom_call_target="tpu_custom_call", output_to_operand_aliasing={{0}: (11, {}), {1}: (12, {}), {2}: (13, {}), {3}: (14, {})} | custom-call | flops 4294967296 | bytes 3145728 | tf_op jit(solution)/shard_map/gated_convs/pallas_call | solution.py:183
  70.4 0.0 copy-start.1
  70.4 3.1 %all-to-all-done.1 = f32[32,8,128]{2,1,0:T(8,128)S(1)} async-done(((f32[32,8,128]{2,1,0:T(8,128)}), f32[32,8,128]{2,1,0:T(8,128)S(1)}, u32[]{:S(2)}, u32[]{:S(2)}) %all-to-all-start.1) | async-done | bytes 131104 | tf_op jit(solution)/shard_map/all_to_all | solution.py:269
  73.5 0.0 copy-done.1
  73.5 2.9 %low_rank.1 = (f32[256,128]{1,0:T(8,128)}, f32[16,128]{1,0:T(8,128)}) custom-call(f32[256,128]{1,0:T(8,128)S(1)} %bitcast.17, f32[16,128]{1,0:T(8,128)S(1)} %bitcast.18), custom_call_target="tpu_custom_call" | custom-call | tf_op jit(solution)/shard_map/low_rank/pallas_call | solution.py:218
  (4 shorter events, 0.0 us)
Async XLA Ops:
  0.6 5.1 %copy-start = (bf16[256,128]{1,0:T(8,128)(2,1)S(1)}, bf16[256,128]{1,0:T(8,128)(2,1)}, u32[]{:S(2)}) copy-start(bf16[256,128]{1,0:T(8,128)(2,1)} %bwd_line.7) | copy-start | bytes 196612
  2.4 8.9 %collective-permute-start = (bf16[128,2048]{1,0:T(8,128)(2,1)S(1)}, bf16[128,2048]{1,0:T(8,128)(2,1)S(1)}, u32[]{:S(2)}, u32[]{:S(2)}) collective-permute-start(bf16[128,2048]{1,0:T(8,128)(2,1)S(1)} %get-tuple-element.59.prod_b.prod_ref), channel_id=1, source_target_pairs={{0,1},{1,2},{2,3},{3,4},{4,5},{5,6},{6,7},{7,8},{8,9},{9,10},{10,1... | collective-permute-start | bytes 1572872 | tf_op jit(solution)/shard_map/ppermute | solution.py:246
  5.1 8.9 %collective-permute-start.1 = (bf16[128,2048]{1,0:T(8,128)(2,1)S(1)}, bf16[128,2048]{1,0:T(8,128)(2,1)S(1)}, u32[]{:S(2)}, u32[]{:S(2)}) collective-permute-start(bf16[128,2048]{1,0:T(8,128)(2,1)S(1)} %get-tuple-element.58.grad_a.grad_ref), channel_id=1, source_target_pairs={{0,63},{1,0},{2,1},{3,2},{4,3},{5,4},{6,5},{7,6},{8,7},{9,8},{10,9... | collective-permute-start | bytes 1572872 | tf_op jit(solution)/shard_map/ppermute | solution.py:243
  6.0 8.1 %copy-start.2 = (bf16[256,256]{1,0:T(8,128)(2,1)S(1)}, bf16[256,256]{1,0:T(8,128)(2,1)}, u32[]{:S(2)}) copy-start(bf16[256,256]{1,0:T(8,128)(2,1)} %constant.28.clone.mask_ref) | copy-start | bytes 393220
  6.0 8.0 %copy-start.3 = (f32[256,128]{1,0:T(8,128)S(1)}, f32[256,128]{1,0:T(8,128)}, u32[]{:S(2)}) copy-start(f32[256,128]{1,0:T(8,128)} %constant.30.clone.turn_ref) | copy-start | bytes 393220
  6.0 8.0 %copy-start.4 = (bf16[128,128]{1,0:T(8,128)(2,1)S(1)}, bf16[128,128]{1,0:T(8,128)(2,1)}, u32[]{:S(2)}) copy-start(bf16[128,128]{1,0:T(8,128)(2,1)} %constant.29.clone.flip_ref) | copy-start | bytes 98308
  21.2 16.7 %all-to-all-start = ((f32[32,8,128]{2,1,0:T(8,128)}), f32[32,8,128]{2,1,0:T(8,128)S(1)}, u32[]{:S(2)}, u32[]{:S(2)}) async-start(f32[32,8,128]{2,1,0:T(8,128)} %bitcast.6), calls=%async_computation | async-start | bytes 262144 | tf_op jit(solution)/shard_map/all_to_all | solution.py:269
  30.2 23.0 %collective-permute-start.5 = (bf16[128,2048]{1,0:T(8,128)(2,1)S(1)}, bf16[128,2048]{1,0:T(8,128)(2,1)}, u32[]{:S(2)}, u32[]{:S(2)}) collective-permute-start(bf16[128,2048]{1,0:T(8,128)(2,1)S(1)} %get-tuple-element.84.prod_a.prod_ref), channel_id=1, source_target_pairs={{0,1},{1,2},{2,3},{3,4},{4,5},{5,6},{6,7},{7,8},{8,9},{9,10},{10,1... | collective-permute-start | bytes 1572872 | tf_op jit(solution)/shard_map/ppermute | solution.py:246
  31.9 21.3 %collective-permute-start.6 = (bf16[128,2048]{1,0:T(8,128)(2,1)S(1)}, bf16[128,2048]{1,0:T(8,128)(2,1)}, u32[]{:S(2)}, u32[]{:S(2)}) collective-permute-start(bf16[128,2048]{1,0:T(8,128)(2,1)S(1)} %get-tuple-element.85.grad_b.grad_ref), channel_id=1, source_target_pairs={{0,63},{1,0},{2,1},{3,2},{4,3},{5,4},{6,5},{7,6},{8,7},{9,8},{10,9... | collective-permute-start | bytes 1572872 | tf_op jit(solution)/shard_map/ppermute | solution.py:243
  37.9 6.7 %collective-permute-start.2 = (f32[8,128]{1,0:T(8,128)S(1)}, f32[8,128]{1,0:T(8,128)S(1)}, u32[]{:S(2)}, u32[]{:S(2)}) collective-permute-start(f32[8,128]{1,0:T(8,128)S(1)} %bitcast_reduce_fusion), channel_id=1, source_target_pairs={{0,8},{8,0},{16,24},{24,16},{32,40},{40,32},{48,56},{56,48},{1,9},... | collective-permute-start | bytes 12296 | tf_op jit(solution)/shard_map/ppermute | solution.py:273
  44.6 6.5 %collective-permute-start.3 = (f32[8,128]{1,0:T(8,128)S(1)}, f32[8,128]{1,0:T(8,128)S(1)}, u32[]{:S(2)}, u32[]{:S(2)}) collective-permute-start(f32[8,128]{1,0:T(8,128)S(1)} %add.17), channel_id=1, source_target_pairs={{0,16},{8,24},{16,0},{24,8},{32,48},{40,56},{48,32},{56,40},{1,17}... | collective-permute-start | bytes 12296 | tf_op jit(solution)/shard_map/ppermute | solution.py:273
  51.1 6.6 %collective-permute-start.4 = (f32[8,128]{1,0:T(8,128)S(1)}, f32[8,128]{1,0:T(8,128)S(1)}, u32[]{:S(2)}, u32[]{:S(2)}) collective-permute-start(f32[8,128]{1,0:T(8,128)S(1)} %add.18), channel_id=1, source_target_pairs={{0,32},{8,40},{16,48},{24,56},{32,0},{40,8},{48,16},{56,24},{1,33}... | collective-permute-start | bytes 12296 | tf_op jit(solution)/shard_map/ppermute | solution.py:273
  58.4 15.1 %all-to-all-start.1 = ((f32[32,8,128]{2,1,0:T(8,128)}), f32[32,8,128]{2,1,0:T(8,128)S(1)}, u32[]{:S(2)}, u32[]{:S(2)}) async-start(f32[32,8,128]{2,1,0:T(8,128)} %broadcast_in_dim.18), calls=%async_computation.1 | async-start | bytes 262144 | tf_op jit(solution)/shard_map/all_to_all | solution.py:269
  70.4 3.1 %copy-start.1 = (f32[128,16]{0,1:T(8,128)S(1)}, f32[128,16]{0,1:T(8,128)}, u32[]{:S(2)}) copy-start(f32[128,16]{0,1:T(8,128)} %param.14) | copy-start | bytes 24580

commit v3 on v2

--- a/solution.py
+++ b/solution.py
@@ -223,7 +223,7 @@
         ],
         compiler_params=pltpu.CompilerParams(vmem_limit_bytes=VMEM_LIMIT),
         name="low_rank",
-    )(grad, basis)
+    )(grad, off_chip(basis))
 
 
 def tie(*arrays):

time: 76.8 us -> 77.5 us (level)
  transfers between devices with their start and end apart: 9 -> 9, of which waited for: 5 -> 5; matrix products, arithmetic and copies ran while one was open for 0% -> 0% of each run, Pallas kernels for 26% -> 25%
where the time goes in v3:
time: 77.5 us; the launch traced here: 77.1 us
  Pallas kernels  32.1 us (41%)
  starting transfers between devices  31.3 us (40%)
  waiting for transfers between devices  11.9 us (15%)
  local copies, waits for them, and re-layouts  0.89 us (1%)
    pallas_call x4, Pallas kernels, gated_convs(): pl.pallas_call(functools.partial(conv_kernel, start * STEP, blocked), gri...  17.9 us
    all_to_all x2, starting transfers between devices, exchanged(): return lax.all_to_all(x, near, 0, 0, tiled=True)  16.4 us
    ppermute x3, starting transfers between devices, hop(): return lambda x: lax.ppermute(x, 'z', route)  9.84 us
    pallas_call x1, Pallas kernels, lag_sums(): pl.pallas_call(lag_kernel, in_specs=[pl.BlockSpec(memory_space=pltpu.SMEM...  7.15 us
    all_to_all x2, waiting for transfers between devices, exchanged(): return lax.all_to_all(x, near, 0, 0, tiled=True)  4.74 us
    ppermute x2, starting transfers between devices, from_last(): return lax.ppermute(x, seq, [(i, (i + 1) % size) for i in range(size)])  4.47 us
    pallas_call x1, Pallas kernels, low_rank(): pl.pallas_call(functools.partial(low_rank_kernel, scale), out_shape=[jax....  3.57 us
    pallas_call x2, Pallas kernels, gated(): pl.pallas_call(gate_kernel, grid=(steps,), in_specs=[grad_at, grad_at, pr...  3.46 us
  transfers between devices with their start and end apart: 9, of which 5 were waited for; matrix products, arithmetic and copies ran while one was open for 0% of the time, Pallas kernels for 25%

profile of v3, /device:TPU:1, one launch (start us, length us, event | category | flops | bytes accessed | tf_op | source)
XLA Modules:
  0.0 77.1 jit_solution(2028261644510641584)
XLA Ops:
  0.6 0.0 copy-start
  0.6 1.7 %gated.2 = (bf16[128,2048]{1,0:T(8,128)(2,1)S(1)}, bf16[128,2048]{1,0:T(8,128)(2,1)S(1)}) custom-call(bf16[128,4096]{1,0:T(8,128)(2,1)} %bitcast.18, bf16[128,4096]{1,0:T(8,128)(2,1)} %bitcast.24, bf16[128,4096]{1,0:T(8,128)(2,1)} %bitcast.30, bf16[128,4096]{1,0:T(8,128)(2,1)} %bitcast.36), custom_call_target="tpu_custom_call" | custom-call | flops 524288 | bytes 3145728 | tf_op jit(solution)/shard_map/gated/pallas_call | solution.py:45
  2.4 2.8 %collective-permute-start = (bf16[128,2048]{1,0:T(8,128)(2,1)S(1)}, bf16[128,2048]{1,0:T(8,128)(2,1)S(1)}, u32[]{:S(2)}, u32[]{:S(2)}) collective-permute-start(bf16[128,2048]{1,0:T(8,128)(2,1)S(1)} %get-tuple-element.59.prod_b.prod_ref), channel_id=1, source_target_pairs={{0,1},{1,2},{2,3},{3,4},{4,5},{5,6},{6,7},{7,8},{8,9},{9,10},{10,1... | collective-permute-start | bytes 1572872 | tf_op jit(solution)/shard_map/ppermute | solution.py:246
  5.1 0.6 collective-permute-start.1
  5.8 0.0 copy-done
  5.8 0.2 rev.3.fwd_line
  6.0 0.0 copy-start.1
  6.0 0.0 copy-start.2
  6.0 0.0 copy-start.3
  6.0 1.8 %gated.3 = (bf16[128,2048]{1,0:T(8,128)(2,1)S(1)}, bf16[128,2048]{1,0:T(8,128)(2,1)S(1)}) custom-call(bf16[128,4096]{1,0:T(8,128)(2,1)} %bitcast.19, bf16[128,4096]{1,0:T(8,128)(2,1)} %bitcast.25, bf16[128,4096]{1,0:T(8,128)(2,1)} %bitcast.31, bf16[128,4096]{1,0:T(8,128)(2,1)} %bitcast.37), custom_call_target="tpu_custom_call" | custom-call | flops 524288 | bytes 3145728 | tf_op jit(solution)/shard_map/gated/pallas_call | solution.py:45
  7.8 0.1 add_convert_fusion.keep_ref
  7.9 3.4 %collective-permute-done.before_ref = bf16[128,2048]{1,0:T(8,128)(2,1)S(1)} collective-permute-done((bf16[128,2048]{1,0:T(8,128)(2,1)S(1)}, bf16[128,2048]{1,0:T(8,128)(2,1)S(1)}, u32[]{:S(2)}, u32[]{:S(2)}) %collective-permute-start) | collective-permute-done | bytes 524320 | tf_op jit(solution)/shard_map/ppermute | solution.py:246
  11.2 2.8 %collective-permute-done.1.after_ref = bf16[128,2048]{1,0:T(8,128)(2,1)S(1)} collective-permute-done((bf16[128,2048]{1,0:T(8,128)(2,1)S(1)}, bf16[128,2048]{1,0:T(8,128)(2,1)S(1)}, u32[]{:S(2)}, u32[]{:S(2)}) %collective-permute-start.1) | collective-permute-done | bytes 524320 | tf_op jit(solution)/shard_map/ppermute | solution.py:243
  14.0 0.0 copy-done.1
  14.0 0.0 copy-done.2
  14.0 0.0 copy-done.3
  14.0 7.1 %lag_sums.1 = f32[256,128]{1,0:T(8,128)} custom-call(f32[2]{0:T(128)S(1)} %add_convert_fusion.keep_ref, bf16[128,2048]{1,0:T(8,128)(2,1)S(1)} %get-tuple-element.59.prod_b.prod_ref, bf16[128,2048]{1,0:T(8,128)(2,1)S(1)} %get-tuple-element.85.grad_b.grad_ref, bf16[128,2048]{1,0:T(8,128)(2,1)S(1)} %collective-permute-done.before_ref, ...), custom_call_target="tpu_custom_call" | custom-call | flops 4294967296 | bytes 3145728 | tf_op jit(solution)/shard_map/lag_sums/pallas_call | solution.py:104
  21.2 9.0 %all-to-all-start = ((f32[32,8,128]{2,1,0:T(8,128)}), f32[32,8,128]{2,1,0:T(8,128)S(1)}, u32[]{:S(2)}, u32[]{:S(2)}) async-start(f32[32,8,128]{2,1,0:T(8,128)} %bitcast.6), calls=%async_computation | async-start | bytes 262144 | tf_op jit(solution)/shard_map/all_to_all | solution.py:269
  30.2 1.7 %collective-permute-start.5 = (bf16[128,2048]{1,0:T(8,128)(2,1)S(1)}, bf16[128,2048]{1,0:T(8,128)(2,1)}, u32[]{:S(2)}, u32[]{:S(2)}) collective-permute-start(bf16[128,2048]{1,0:T(8,128)(2,1)S(1)} %get-tuple-element.84.prod_a.prod_ref), channel_id=1, source_target_pairs={{0,1},{1,2},{2,3},{3,4},{4,5},{5,6},{6,7},{7,8},{8,9},{9,10},{10,1... | collective-permute-start | bytes 1572872 | tf_op jit(solution)/shard_map/ppermute | solution.py:246
  31.9 0.0 collective-permute-start.6
  31.9 4.4 %gated_convs.4 = (bf16[128,4096]{1,0:T(8,128)(2,1)}, bf16[128,4096]{1,0:T(8,128)(2,1)}, bf16[128,4096]{1,0:T(8,128)(2,1)}, bf16[128,4096]{1,0:T(8,128)(2,1)}) custom-call(f32[2]{0:T(128)S(1)} %add_convert_fusion.keep_ref, bf16[256,128]{1,0:T(8,128)(2,1)S(1)} %rev.3.fwd_line, bf16[128,2048]{1,0:T(8,128)(2,1)S(1)} %get-tuple-element.59.prod_b.prod_ref, ...), custom_call_target="tpu_custom_call" | custom-call | flops 4294967296 | bytes 3145728 | tf_op jit(solution)/shard_map/gated_convs/pallas_call | solution.py:183
  36.3 1.6 %all-to-all-done = f32[32,8,128]{2,1,0:T(8,128)S(1)} async-done(((f32[32,8,128]{2,1,0:T(8,128)}), f32[32,8,128]{2,1,0:T(8,128)S(1)}, u32[]{:S(2)}, u32[]{:S(2)}) %all-to-all-start) | async-done | bytes 131104 | tf_op jit(solution)/shard_map/all_to_all | solution.py:269
  37.9 2.3 %collective-permute-start.2 = (f32[8,128]{1,0:T(8,128)S(1)}, f32[8,128]{1,0:T(8,128)S(1)}, u32[]{:S(2)}, u32[]{:S(2)}) collective-permute-start(f32[8,128]{1,0:T(8,128)S(1)} %bitcast_reduce_fusion), channel_id=1, source_target_pairs={{0,8},{8,0},{16,24},{24,16},{32,40},{40,32},{48,56},{56,48},{1,9},... | collective-permute-start | bytes 12296 | tf_op jit(solution)/shard_map/ppermute | solution.py:273
  40.2 4.4 %gated_convs.5 = (bf16[128,4096]{1,0:T(8,128)(2,1)}, bf16[128,4096]{1,0:T(8,128)(2,1)}, bf16[128,4096]{1,0:T(8,128)(2,1)}, bf16[128,4096]{1,0:T(8,128)(2,1)}) custom-call(f32[2]{0:T(128)S(1)} %add_convert_fusion.keep_ref, bf16[256,128]{1,0:T(8,128)(2,1)S(1)} %rev.3.fwd_line, ...), custom_call_target="tpu_custom_call", output_to_operand_aliasing={{0}: (11, {}), {1}: (12, {}), {2}: (13, {}), {3}: (14, {})} | custom-call | flops 4294967296 | bytes 3145728 | tf_op jit(solution)/shard_map/gated_convs/pallas_call | solution.py:183
  44.6 0.0 collective-permute-done.2
  44.6 5.5 %collective-permute-start.3 = (f32[8,128]{1,0:T(8,128)S(1)}, f32[8,128]{1,0:T(8,128)S(1)}, u32[]{:S(2)}, u32[]{:S(2)}) collective-permute-start(f32[8,128]{1,0:T(8,128)S(1)} %add.17), channel_id=1, source_target_pairs={{0,16},{8,24},{16,0},{24,8},{32,48},{40,56},{48,32},{56,40},{1,17}... | collective-permute-start | bytes 12296 | tf_op jit(solution)/shard_map/ppermute | solution.py:273
  50.1 1.0 %collective-permute-done.3 = f32[8,128]{1,0:T(8,128)S(1)} collective-permute-done((f32[8,128]{1,0:T(8,128)S(1)}, f32[8,128]{1,0:T(8,128)S(1)}, u32[]{:S(2)}, u32[]{:S(2)}) %collective-permute-start.3) | collective-permute-done | bytes 4128 | tf_op jit(solution)/shard_map/ppermute | solution.py:273
  51.1 2.1 %collective-permute-start.4 = (f32[8,128]{1,0:T(8,128)S(1)}, f32[8,128]{1,0:T(8,128)S(1)}, u32[]{:S(2)}, u32[]{:S(2)}) collective-permute-start(f32[8,128]{1,0:T(8,128)S(1)} %add.18), channel_id=1, source_target_pairs={{0,32},{8,40},{16,48},{24,56},{32,0},{40,8},{48,16},{56,24},{1,33}... | collective-permute-start | bytes 12296 | tf_op jit(solution)/shard_map/ppermute | solution.py:273
  53.2 0.0 collective-permute-done.5.before_ref
  53.2 0.0 collective-permute-done.6.after_ref
  53.2 4.6 %gated_convs.6 = (bf16[128,4096]{1,0:T(8,128)(2,1)}, bf16[128,4096]{1,0:T(8,128)(2,1)}, bf16[128,4096]{1,0:T(8,128)(2,1)}, bf16[128,4096]{1,0:T(8,128)(2,1)}) custom-call(f32[2]{0:T(128)S(1)} %add_convert_fusion.keep_ref, bf16[256,128]{1,0:T(8,128)(2,1)S(1)} %rev.3.fwd_line, ...), custom_call_target="tpu_custom_call", output_to_operand_aliasing={{0}: (11, {}), {1}: (12, {}), {2}: (13, {}), {3}: (14, {})} | custom-call | flops 4294967296 | bytes 3145728 | tf_op jit(solution)/shard_map/gated_convs/pallas_call | solution.py:183
  57.7 0.0 collective-permute-done.4
  57.7 0.7 broadcast_in_dim.18
  58.4 7.4 %all-to-all-start.1 = ((f32[32,8,128]{2,1,0:T(8,128)}), f32[32,8,128]{2,1,0:T(8,128)S(1)}, u32[]{:S(2)}, u32[]{:S(2)}) async-start(f32[32,8,128]{2,1,0:T(8,128)} %broadcast_in_dim.18), calls=%async_computation.1 | async-start | bytes 262144 | tf_op jit(solution)/shard_map/all_to_all | solution.py:269
  65.8 4.6 %gated_convs.7 = (bf16[128,4096]{1,0:T(8,128)(2,1)}, bf16[128,4096]{1,0:T(8,128)(2,1)}, bf16[128,4096]{1,0:T(8,128)(2,1)}, bf16[128,4096]{1,0:T(8,128)(2,1)}) custom-call(f32[2]{0:T(128)S(1)} %add_convert_fusion.keep_ref, bf16[256,128]{1,0:T(8,128)(2,1)S(1)} %rev.3.fwd_line, ...), custom_call_target="tpu_custom_call", output_to_operand_aliasing={{0}: (11, {}), {1}: (12, {}), {2}: (13, {}), {3}: (14, {})} | custom-call | flops 4294967296 | bytes 3145728 | tf_op jit(solution)/shard_map/gated_convs/pallas_call | solution.py:183
  70.4 3.1 %all-to-all-done.1 = f32[32,8,128]{2,1,0:T(8,128)S(1)} async-done(((f32[32,8,128]{2,1,0:T(8,128)}), f32[32,8,128]{2,1,0:T(8,128)S(1)}, u32[]{:S(2)}, u32[]{:S(2)}) %all-to-all-start.1) | async-done | bytes 131104 | tf_op jit(solution)/shard_map/all_to_all | solution.py:269
  73.5 3.6 %low_rank.1 = (f32[256,128]{1,0:T(8,128)}, f32[16,128]{1,0:T(8,128)}) custom-call(f32[256,128]{1,0:T(8,128)S(1)} %bitcast.17, f32[16,128]{1,0:T(8,128)} %bitcast.43), custom_call_target="tpu_custom_call" | custom-call | tf_op jit(solution)/shard_map/low_rank/pallas_call | solution.py:218
  (4 shorter events, 0.0 us)
Async XLA Ops:
  0.6 5.1 %copy-start = (bf16[256,128]{1,0:T(8,128)(2,1)S(1)}, bf16[256,128]{1,0:T(8,128)(2,1)}, u32[]{:S(2)}) copy-start(bf16[256,128]{1,0:T(8,128)(2,1)} %bwd_line.7) | copy-start | bytes 196612
  2.4 8.9 %collective-permute-start = (bf16[128,2048]{1,0:T(8,128)(2,1)S(1)}, bf16[128,2048]{1,0:T(8,128)(2,1)S(1)}, u32[]{:S(2)}, u32[]{:S(2)}) collective-permute-start(bf16[128,2048]{1,0:T(8,128)(2,1)S(1)} %get-tuple-element.59.prod_b.prod_ref), channel_id=1, source_target_pairs={{0,1},{1,2},{2,3},{3,4},{4,5},{5,6},{6,7},{7,8},{8,9},{9,10},{10,1... | collective-permute-start | bytes 1572872 | tf_op jit(solution)/shard_map/ppermute | solution.py:246
  5.1 8.9 %collective-permute-start.1 = (bf16[128,2048]{1,0:T(8,128)(2,1)S(1)}, bf16[128,2048]{1,0:T(8,128)(2,1)S(1)}, u32[]{:S(2)}, u32[]{:S(2)}) collective-permute-start(bf16[128,2048]{1,0:T(8,128)(2,1)S(1)} %get-tuple-element.58.grad_a.grad_ref), channel_id=1, source_target_pairs={{0,63},{1,0},{2,1},{3,2},{4,3},{5,4},{6,5},{7,6},{8,7},{9,8},{10,9... | collective-permute-start | bytes 1572872 | tf_op jit(solution)/shard_map/ppermute | solution.py:243
  6.0 8.1 %copy-start.1 = (bf16[256,256]{1,0:T(8,128)(2,1)S(1)}, bf16[256,256]{1,0:T(8,128)(2,1)}, u32[]{:S(2)}) copy-start(bf16[256,256]{1,0:T(8,128)(2,1)} %constant.28.clone.mask_ref) | copy-start | bytes 393220
  6.0 8.0 %copy-start.2 = (f32[256,128]{1,0:T(8,128)S(1)}, f32[256,128]{1,0:T(8,128)}, u32[]{:S(2)}) copy-start(f32[256,128]{1,0:T(8,128)} %constant.30.clone.turn_ref) | copy-start | bytes 393220
  6.0 8.0 %copy-start.3 = (bf16[128,128]{1,0:T(8,128)(2,1)S(1)}, bf16[128,128]{1,0:T(8,128)(2,1)}, u32[]{:S(2)}) copy-start(bf16[128,128]{1,0:T(8,128)(2,1)} %constant.29.clone.flip_ref) | copy-start | bytes 98308
  21.2 16.7 %all-to-all-start = ((f32[32,8,128]{2,1,0:T(8,128)}), f32[32,8,128]{2,1,0:T(8,128)S(1)}, u32[]{:S(2)}, u32[]{:S(2)}) async-start(f32[32,8,128]{2,1,0:T(8,128)} %bitcast.6), calls=%async_computation | async-start | bytes 262144 | tf_op jit(solution)/shard_map/all_to_all | solution.py:269
  30.2 23.0 %collective-permute-start.5 = (bf16[128,2048]{1,0:T(8,128)(2,1)S(1)}, bf16[128,2048]{1,0:T(8,128)(2,1)}, u32[]{:S(2)}, u32[]{:S(2)}) collective-permute-start(bf16[128,2048]{1,0:T(8,128)(2,1)S(1)} %get-tuple-element.84.prod_a.prod_ref), channel_id=1, source_target_pairs={{0,1},{1,2},{2,3},{3,4},{4,5},{5,6},{6,7},{7,8},{8,9},{9,10},{10,1... | collective-permute-start | bytes 1572872 | tf_op jit(solution)/shard_map/ppermute | solution.py:246
  31.9 21.3 %collective-permute-start.6 = (bf16[128,2048]{1,0:T(8,128)(2,1)S(1)}, bf16[128,2048]{1,0:T(8,128)(2,1)}, u32[]{:S(2)}, u32[]{:S(2)}) collective-permute-start(bf16[128,2048]{1,0:T(8,128)(2,1)S(1)} %get-tuple-element.85.grad_b.grad_ref), channel_id=1, source_target_pairs={{0,63},{1,0},{2,1},{3,2},{4,3},{5,4},{6,5},{7,6},{8,7},{9,8},{10,9... | collective-permute-start | bytes 1572872 | tf_op jit(solution)/shard_map/ppermute | solution.py:243
  37.9 6.7 %collective-permute-start.2 = (f32[8,128]{1,0:T(8,128)S(1)}, f32[8,128]{1,0:T(8,128)S(1)}, u32[]{:S(2)}, u32[]{:S(2)}) collective-permute-start(f32[8,128]{1,0:T(8,128)S(1)} %bitcast_reduce_fusion), channel_id=1, source_target_pairs={{0,8},{8,0},{16,24},{24,16},{32,40},{40,32},{48,56},{56,48},{1,9},... | collective-permute-start | bytes 12296 | tf_op jit(solution)/shard_map/ppermute | solution.py:273
  44.6 6.5 %collective-permute-start.3 = (f32[8,128]{1,0:T(8,128)S(1)}, f32[8,128]{1,0:T(8,128)S(1)}, u32[]{:S(2)}, u32[]{:S(2)}) collective-permute-start(f32[8,128]{1,0:T(8,128)S(1)} %add.17), channel_id=1, source_target_pairs={{0,16},{8,24},{16,0},{24,8},{32,48},{40,56},{48,32},{56,40},{1,17}... | collective-permute-start | bytes 12296 | tf_op jit(solution)/shard_map/ppermute | solution.py:273
  51.1 6.6 %collective-permute-start.4 = (f32[8,128]{1,0:T(8,128)S(1)}, f32[8,128]{1,0:T(8,128)S(1)}, u32[]{:S(2)}, u32[]{:S(2)}) collective-permute-start(f32[8,128]{1,0:T(8,128)S(1)} %add.18), channel_id=1, source_target_pairs={{0,32},{8,40},{16,48},{24,56},{32,0},{40,8},{48,16},{56,24},{1,33}... | collective-permute-start | bytes 12296 | tf_op jit(solution)/shard_map/ppermute | solution.py:273
  58.4 15.1 %all-to-all-start.1 = ((f32[32,8,128]{2,1,0:T(8,128)}), f32[32,8,128]{2,1,0:T(8,128)S(1)}, u32[]{:S(2)}, u32[]{:S(2)}) async-start(f32[32,8,128]{2,1,0:T(8,128)} %broadcast_in_dim.18), calls=%async_computation.1 | async-start | bytes 262144 | tf_op jit(solution)/shard_map/all_to_all | solution.py:269
